TPU v7x, 128 devices: a whole 4x4x4 slice. The times are simulated.
128 devices in a mesh: shard: 16 (over y, z), tp: 8 (over x, core).
Axes of the slice: x: 4, y: 4, z: 4, core: 2. Of those that a mesh axis runs over, the one named last changes fastest.
Arguments:
- gradient: bfloat16 [4096, 16384], P('shard', 'tp'), may hold values from -2 to 2
- table: int32 [256, 3], replicated, may hold values from 0 to 127, as said below
- left_stat: bfloat16 [384, 512, 512], P(('shard', 'tp')), as said below
- right_stat: bfloat16 [384, 512, 512], P(('shard', 'tp')), as said below
- left_basis: bfloat16 [384, 512, 512], P(('shard', 'tp')), may hold values from -0.25 to 0.25
- right_basis: bfloat16 [384, 512, 512], P(('shard', 'tp')), may hold values from -0.25 to 0.25
- moment: bfloat16 [384, 512, 512], P(('shard', 'tp')), may hold values from -2 to 2
- second: float32 [384, 512, 512], P(('shard', 'tp')), may hold values from 0.02 to 0.2
Outputs:
- update: bfloat16 [4096, 16384], P('shard', 'tp')
- new_left: bfloat16 [384, 512, 512], P(('shard', 'tp'))
- new_right: bfloat16 [384, 512, 512], P(('shard', 'tp'))
- new_moment: bfloat16 [384, 512, 512], P(('shard', 'tp'))
- new_second: float32 [384, 512, 512], P(('shard', 'tp'))
Inputs may be any that keep to these rules, and one draw needn't show every extreme that they name: `table`: column 0 is a block row below 8, column 1 a block column below 32, column 2 an owner device below 128; every block appears in exactly one row; each device owns between 1 and 3 blocks, and some device owns exactly 3. `left_stat`: Symmetric. `right_stat`: Symmetric.
All inputs are finite; a program needn't handle non-finite values.
Results may differ from a plain program's by a relative error of at most 0.0085.
Values may be sent and summed in bfloat16 or wider, within the bound.
No kernel may reach another device: no remote copies, remote signals or barrier semaphores. Data moves between devices by JAX's collectives and lax.ppermute only.
A program may use at most 128 MiB of HBM per device.

v0:
```python
import jax
import jax.numpy as jnp
from jax import lax
from jax.sharding import PartitionSpec as P

beta_moment = 0.9
beta_second = 0.95
beta_stats = 0.95
epsilon = 1e-08


def slot_table(table, slots):
    owners = table[:, 2]
    count = owners.shape[0]
    order = jnp.arange(count, dtype=jnp.int32)
    earlier = (owners[None, :] == owners[:, None]) & (order[None, :] < order[:, None])
    slot_rank = jnp.sum(earlier.astype(jnp.int32), axis=1)
    return owners * slots + slot_rank


def move_grad(array):
    return lax.all_to_all(array, ("shard", "tp"), split_axis=1, concat_axis=1, tiled=True)


def move_blocks(array):
    return lax.all_to_all(array, ("shard", "tp"), split_axis=2, concat_axis=2, tiled=True)


def move_updates(array):
    return lax.all_to_all(array, ("shard", "tp"), split_axis=2, concat_axis=2, tiled=True)


def move_stripes(array):
    return lax.all_to_all(array, ("shard", "tp"), split_axis=1, concat_axis=1, tiled=True)


def precondition_slots(grad_blocks, left, right, left_q, right_q, first, squares):
    left_new = (
        beta_stats * left.astype(jnp.float32)
        + (1.0 - beta_stats)
        * jnp.einsum("sik,sjk->sij", grad_blocks, grad_blocks, preferred_element_type=jnp.float32)
    ).astype(jnp.bfloat16)
    right_new = (
        beta_stats * right.astype(jnp.float32)
        + (1.0 - beta_stats)
        * jnp.einsum("ski,skj->sij", grad_blocks, grad_blocks, preferred_element_type=jnp.float32)
    ).astype(jnp.bfloat16)
    first_new = (
        beta_moment * first.astype(jnp.float32)
        + (1.0 - beta_moment) * grad_blocks.astype(jnp.float32)
    ).astype(jnp.bfloat16)
    left_grad = jnp.einsum(
        "ski,skj->sij", left_q, grad_blocks, preferred_element_type=jnp.float32
    ).astype(jnp.bfloat16)
    left_first = jnp.einsum(
        "ski,skj->sij", left_q, first_new, preferred_element_type=jnp.float32
    ).astype(jnp.bfloat16)
    rotated = jnp.einsum("sij,sjk->sik", left_grad, right_q, preferred_element_type=jnp.float32)
    first_rot = jnp.einsum("sij,sjk->sik", left_first, right_q, preferred_element_type=jnp.float32)
    squares_new = beta_second * squares + (1.0 - beta_second) * rotated * rotated
    scaled = (first_rot / (jnp.sqrt(squares_new) + epsilon)).astype(jnp.bfloat16)
    back = jnp.einsum("sij,sjk->sik", left_q, scaled, preferred_element_type=jnp.float32).astype(
        jnp.bfloat16
    )
    result = jnp.einsum("sij,skj->sik", back, right_q, preferred_element_type=jnp.float32).astype(
        jnp.bfloat16
    )
    return (result, left_new, right_new, first_new, squares_new)


def shards(gradient, table, left_stat, right_stat, left_basis, right_basis, moment, second):
    shard_count = lax.axis_size("shard")
    tp_count = lax.axis_size("tp")
    dev_count = shard_count * tp_count
    row_dev, col_dev = gradient.shape
    slots = left_stat.shape[0]
    side = left_stat.shape[1]
    halves = side // row_dev
    block_rows = shard_count // halves
    cols_per_dev = col_dev // side
    block_cols = tp_count * cols_per_dev
    piece_len = row_dev * side // dev_count
    tiled = gradient.reshape(row_dev, cols_per_dev, side).transpose(1, 0, 2)
    received = move_grad(tiled.reshape(cols_per_dev, dev_count, piece_len))
    spread = received.reshape(cols_per_dev, block_rows, halves, tp_count, piece_len)
    state_row = slot_table(table, slots)
    block_id = table[:, 0] * block_cols + table[:, 1]
    targets = jnp.arange(dev_count * slots, dtype=jnp.int32)
    matches = (state_row[None, :] == targets[:, None]).astype(jnp.int32)
    send_id = jnp.sum(matches * block_id[None, :], axis=1)
    filled = jnp.sum(matches, axis=1)
    send_grid = send_id.reshape(dev_count, slots).T
    fill_grid = filled.reshape(dev_count, slots).T
    send_row = (send_grid // block_cols)[:, None, :]
    send_col = send_grid % block_cols
    send_tp = (send_col // cols_per_dev)[:, None, :]
    send_local = (send_col % cols_per_dev)[:, None, :]
    half_index = jnp.arange(halves, dtype=jnp.int32)[None, :, None]
    picked = spread[send_local, send_row, half_index, send_tp]
    outbox = jnp.where(fill_grid[:, None, :, None] > 0, picked, jnp.zeros((), jnp.bfloat16))
    inbox = move_blocks(outbox)
    grad_blocks = inbox.reshape(slots, side, side)
    myself = lax.axis_index(("shard", "tp"))
    mine = lax.dynamic_slice_in_dim(filled, myself * slots, slots)
    results = precondition_slots(
        grad_blocks, left_stat, right_stat, left_basis, right_basis, moment, second
    )
    block_updates, left_new, right_new, first_new, squares_new = results
    retain = mine[:, None, None] > 0
    new_left = jnp.where(retain, left_new, left_stat)
    new_right = jnp.where(retain, right_new, right_stat)
    new_moment = jnp.where(retain, first_new, moment)
    new_second = jnp.where(retain, squares_new, second)
    returned = move_updates(block_updates.reshape(slots, halves, dev_count, piece_len))
    block_count = table.shape[0]
    positions = jnp.arange(block_count, dtype=jnp.int32)
    block_match = (block_id[None, :] == positions[:, None]).astype(jnp.int32)
    slot_of_block = jnp.sum(block_match * state_row[None, :], axis=1)
    local_col = jnp.arange(cols_per_dev, dtype=jnp.int32)[:, None, None, None]
    row_index = jnp.arange(block_rows, dtype=jnp.int32)[None, :, None, None]
    half_grid = jnp.arange(halves, dtype=jnp.int32)[None, None, :, None]
    tp_index = jnp.arange(tp_count, dtype=jnp.int32)[None, None, None, :]
    which = row_index * block_cols + tp_index * cols_per_dev + local_col
    which = jnp.broadcast_to(which, (cols_per_dev, block_rows, halves, tp_count))
    chosen = slot_of_block[which]
    gathered = returned[chosen % slots, half_grid, chosen // slots]
    arrived = move_stripes(gathered.reshape(cols_per_dev, dev_count, piece_len))
    update = (
        arrived.reshape(cols_per_dev, row_dev, side).transpose(1, 0, 2).reshape(row_dev, col_dev)
    )
    return (update, new_left, new_right, new_moment, new_second)


def solution(mesh):
    in_specs = (
        P("shard", "tp"),
        P(),
        P(("shard", "tp"), None, None),
        P(("shard", "tp"), None, None),
        P(("shard", "tp"), None, None),
        P(("shard", "tp"), None, None),
        P(("shard", "tp"), None, None),
        P(("shard", "tp"), None, None),
    )
    out_specs = (
        P("shard", "tp"),
        P(("shard", "tp"), None, None),
        P(("shard", "tp"), None, None),
        P(("shard", "tp"), None, None),
        P(("shard", "tp"), None, None),
    )
    return jax.shard_map(shards, mesh=mesh, in_specs=in_specs, out_specs=out_specs, check_vma=False)
```

profile of v0, /device:TPU:1, one launch (start us, length us, event | category | flops | bytes accessed | tf_op | source)
XLA Modules:
  0.0 183.7 jit_solution(15024660029134863761)
XLA Ops:
  0.6 2.7 %reshape.218 = bf16[256,4,512]{2,1,0:T(4,128)(2,1)} reshape(bf16[256,2048]{1,0:T(8,128)(2,1)} %param.8) | data formatting | bytes 2097152 | tf_op jit(solution)/shard_map/reshape | solution.py:83
  3.4 11.9 %all-to-all-start = ((bf16[4,128,1024]{2,0,1:T(4,128)(2,1)}), bf16[4,128,1024]{2,0,1:T(4,128)(2,1)}, u32[]{:S(2)}, u32[]{:S(2)}) async-start(bf16[4,128,1024]{2,0,1:T(4,128)(2,1)} %bitcast.3), calls=%async_computation | async-start | bytes 2097152 | tf_op jit(solution)/shard_map/all_to_all | solution.py:22
  16.6 17.6 %all-to-all-done = bf16[4,128,1024]{2,0,1:T(4,128)(2,1)} async-done(((bf16[4,128,1024]{2,0,1:T(4,128)(2,1)}), bf16[4,128,1024]{2,0,1:T(4,128)(2,1)}, u32[]{:S(2)}, u32[]{:S(2)}) %all-to-all-start) | async-done | bytes 1048608 | tf_op jit(solution)/shard_map/all_to_all | solution.py:22
  35.8 13.1 %gather_fusion = bf16[768,1024]{1,0:T(8,128)(2,1)} fusion(bf16[4,8,2,8,1024]{4,3,2,1,0:T(8,128)(2,1)S(1)} %bitcast.67, s32[768]{0:T(1024)S(1)} %reshape.227), kind=kCustom, calls=%fused_computation | custom fusion | bytes 3158016 | tf_op jit(solution)/shard_map/gather | solution.py:99
  48.8 4.9 %broadcast_select_fusion = bf16[3,2,128,1024]{3,1,0,2:T(2,128)(2,1)} fusion(pred[3,128]{0,1:T(8,128)(4,1)S(1)} %bitcast.71, bf16[3,2,128,1024]{3,2,1,0:T(8,128)(2,1)} %bitcast.68), kind=kLoop, calls=%fused_computation.9 | loop fusion | flops 786432 | bytes 3146112 | tf_op jit(solution)/shard_map/jit(_where)/select_n | solution.py:100
  53.8 4.4 %all-to-all-start.1 = ((bf16[3,2,128,1024]{3,1,0,2:T(2,128)(2,1)}), bf16[3,2,128,1024]{3,1,0,2:T(2,128)(2,1)S(1)}, u32[]{:S(2)}, u32[]{:S(2)}) async-start(bf16[3,2,128,1024]{3,1,0,2:T(2,128)(2,1)} %broadcast_select_fusion), calls=%async_computation.1 | async-start | bytes 3145728 | tf_op jit(solution)/shard_map/all_to_all | solution.py:26
  58.4 24.8 %all-to-all-done.1 = bf16[3,2,128,1024]{3,1,0,2:T(2,128)(2,1)S(1)} async-done(((bf16[3,2,128,1024]{3,1,0,2:T(2,128)(2,1)}), bf16[3,2,128,1024]{3,1,0,2:T(2,128)(2,1)S(1)}, u32[]{:S(2)}, u32[]{:S(2)}) %all-to-all-start.1) | async-done | bytes 1572896 | tf_op jit(solution)/shard_map/all_to_all | solution.py:26
  84.8 2.4 %reshape.222 = bf16[3,512,512]{2,1,0:T(8,128)(2,1)S(1)} reshape(bf16[3,2,128,1024]{3,2,1,0:T(8,128)(2,1)} %copy.41) | data formatting | bytes 3145728 | tf_op jit(solution)/shard_map/reshape | solution.py:102
  87.2 4.2 %convolution_convert_fusion.3 = bf16[3,512,512]{2,1,0:T(8,128)(2,1)} fusion(bf16[3,512,512]{2,1,0:T(8,128)(2,1)S(1)} %copy-done, bf16[3,512,512]{2,1,0:T(8,128)(2,1)S(1)} %reshape.222, bf16[3,512,512]{2,1,0:T(8,128)(2,1)} %param.14), kind=kOutput, calls=%fused_computation.16 | convolution fusion | flops 810811392 | bytes 6291456 | tf_op jit(solution)/shard_map/ski,skj->sij/dot_general | solution.py:55
  91.4 6.1 %fusion.1 = (f32[3,512,512]{2,1,0:T(8,128)}, f32[3,512,512]{2,1,0:T(8,128)}) fusion(f32[3,512,512]{2,1,0:T(8,128)} %param.15, pred[3]{0:T(512)(128)(4,1)S(1)} %dynamic-slice_compare_fusion, bf16[3,512,512]{2,1,0:T(8,128)(2,1)} %param.13, bf16[3,512,512]{2,1,0:T(8,128)(2,1)S(1)} %reshape.222, bf16[3,512,512]{2,1,0:T(8,128)(2,1)S(1)} %copy-done), kind=kOutput, calls=%fused_computation.10 | convolution fusion | flops 1615331328 | bytes 14155779 | tf_op jit(solution)/shard_map/sij,sjk->sik/dot_general | solution.py:58
  97.5 7.9 %convolution_convert_fusion.1 = bf16[3,512,512]{2,1,0:T(8,128)(2,1)} fusion(bf16[3,512,512]{2,1,0:T(8,128)(2,1)S(1)} %copy-done, f32[3,512,512]{2,1,0:T(8,128)} %get-tuple-element.16, f32[3,512,512]{2,1,0:T(8,128)} %param.15, bf16[3,512,512]{2,1,0:T(8,128)(2,1)} %convolution_convert_fusion.3, bf16[3,512,512]{2,1,0:T(8,128)(2,1)} %param.13), kind=kOutput, calls=%fused_computation.14 | convolution fusion | flops 1616904192 | bytes 12582912 | tf_op jit(solution)/shard_map/sij,sjk->sik/dot_general | solution.py:62
  105.4 3.7 %convolution_convert_fusion = bf16[3,512,512]{2,1,0:T(8,128)(2,1)} fusion(bf16[3,512,512]{2,1,0:T(8,128)(2,1)} %convolution_convert_fusion.1, bf16[3,512,512]{2,1,0:T(8,128)(2,1)S(1)} %copy-done.3), kind=kOutput, calls=%fused_computation.13 | convolution fusion | flops 806092800 | bytes 4718592 | tf_op jit(solution)/shard_map/sij,skj->sik/dot_general | solution.py:65
  109.1 2.4 %reshape.223 = bf16[3,2,128,1024]{3,2,1,0:T(8,128)(2,1)S(1)} reshape(bf16[3,512,512]{2,1,0:T(8,128)(2,1)} %convolution_convert_fusion) | data formatting | bytes 3145728 | tf_op jit(solution)/shard_map/reshape | solution.py:114
  111.6 2.8 %copy.48 = bf16[3,2,128,1024]{3,1,0,2:T(2,128)(2,1)} copy(bf16[3,2,128,1024]{3,2,1,0:T(8,128)(2,1)S(1)} %reshape.223) | data formatting | bytes 3145728 | tf_op jit(solution)/shard_map/reshape | solution.py:114
  114.4 5.4 %all-to-all-start.2 = ((bf16[3,2,128,1024]{3,1,0,2:T(2,128)(2,1)}), bf16[3,2,128,1024]{3,1,0,2:T(2,128)(2,1)}, u32[]{:S(2)}, u32[]{:S(2)}) async-start(bf16[3,2,128,1024]{3,1,0,2:T(2,128)(2,1)} %copy.48), calls=%async_computation.2 | async-start | bytes 3145728 | tf_op jit(solution)/shard_map/all_to_all | solution.py:30
  120.1 3.5 %gather_fusion.1 = s32[512]{0:T(512)S(1)} fusion(s32[256]{0:T(256)S(1)} %select_reduce_fusion.1, s32[1024]{0:T(1024)S(1)} %pad_clamp_fusion), kind=kCustom, calls=%fused_computation.1 | custom fusion | bytes 6144 | tf_op jit(solution)/shard_map/gather | solution.py:125
  124.2 20.3 %all-to-all-done.2 = bf16[3,2,128,1024]{3,1,0,2:T(2,128)(2,1)} async-done(((bf16[3,2,128,1024]{3,1,0,2:T(2,128)(2,1)}), bf16[3,2,128,1024]{3,1,0,2:T(2,128)(2,1)}, u32[]{:S(2)}, u32[]{:S(2)}) %all-to-all-start.2) | async-done | bytes 1572896 | tf_op jit(solution)/shard_map/all_to_all | solution.py:30
  146.3 7.2 %gather_fusion.2 = bf16[512,1024]{1,0:T(8,128)(2,1)} fusion(bf16[3,2,128,1024]{3,2,1,0:T(8,128)(2,1)S(1)} %copy.49, s32[512]{0:T(512)S(1)} %reshape.241), kind=kCustom, calls=%fused_computation.2 | custom fusion | bytes 2103296 | tf_op jit(solution)/shard_map/gather | solution.py:126
  153.6 3.1 %copy.50 = bf16[4,128,1024]{2,0,1:T(4,128)(2,1)} copy(bf16[4,128,1024]{2,1,0:T(8,128)(2,1)} %bitcast.69) | data formatting | bytes 2097152 | tf_op jit(solution)/shard_map/reshape | solution.py:127
  156.6 5.6 %all-to-all-start.3 = ((bf16[4,128,1024]{2,0,1:T(4,128)(2,1)}), bf16[4,128,1024]{2,0,1:T(4,128)(2,1)}, u32[]{:S(2)}, u32[]{:S(2)}) async-start(bf16[4,128,1024]{2,0,1:T(4,128)(2,1)} %copy.50), calls=%async_computation.3 | async-start | bytes 2097152 | tf_op jit(solution)/shard_map/all_to_all | solution.py:34
  162.2 4.0 %broadcast_select_fusion.1 = bf16[3,512,512]{2,1,0:T(8,128)(2,1)} fusion(bf16[3,512,512]{2,1,0:T(8,128)(2,1)} %param.14, pred[3]{0:T(512)(128)(4,1)S(1)} %dynamic-slice_compare_fusion, bf16[3,512,512]{2,1,0:T(8,128)(2,1)S(1)} %copy-done.2), kind=kLoop, calls=%fused_computation.17 | loop fusion | flops 5505024 | bytes 4718595 | tf_op jit(solution)/shard_map/jit(_where)/select_n | solution.py:112
  166.2 2.6 %fusion.3 = bf16[3,512,512]{2,1,0:T(8,128)(2,1)} fusion(bf16[3,512,512]{2,1,0:T(8,128)(2,1)S(1)} %copy-done.5, bf16[3,512,512]{2,1,0:T(8,128)(2,1)S(1)} %copy-done.2, pred[3]{0:T(512)(128)(4,1)S(1)} %dynamic-slice_compare_fusion), kind=kOutput, calls=%fused_computation.12 | convolution fusion | flops 810024960 | bytes 4718595 | tf_op jit(solution)/shard_map/ski,skj->sij/dot_general | solution.py:46
  171.1 10.1 %all-to-all-done.3 = bf16[4,128,1024]{2,0,1:T(4,128)(2,1)} async-done(((bf16[4,128,1024]{2,0,1:T(4,128)(2,1)}), bf16[4,128,1024]{2,0,1:T(4,128)(2,1)}, u32[]{:S(2)}, u32[]{:S(2)}) %all-to-all-start.3) | async-done | bytes 1048608 | tf_op jit(solution)/shard_map/all_to_all | solution.py:34
  181.2 2.5 %copy.60 = bf16[32,8,4,512]{3,1,2,0:T(8,128)(2,1)} copy(bf16[32,8,4,512]{3,2,1,0:T(4,128)(2,1)} %bitcast.18) | data formatting | bytes 2097152
  (46 shorter events, 9.5 us)
Async XLA Ops:
  0.6 86.6 %copy-start = (bf16[3,512,512]{2,1,0:T(8,128)(2,1)S(1)}, bf16[3,512,512]{2,1,0:T(8,128)(2,1)}, u32[]{:S(2)}) copy-start(bf16[3,512,512]{2,1,0:T(8,128)(2,1)} %param.12) | copy-start | bytes 4718596
  3.4 12.0 %copy-start.4 = (s32[256,3]{0,1:T(4,128)S(1)}, s32[256,3]{0,1:T(4,128)}, u32[]{:S(2)}) copy-start(s32[256,3]{0,1:T(4,128)} %param.9) | copy-start | bytes 9220
  3.4 30.8 %all-to-all-start = ((bf16[4,128,1024]{2,0,1:T(4,128)(2,1)}), bf16[4,128,1024]{2,0,1:T(4,128)(2,1)}, u32[]{:S(2)}, u32[]{:S(2)}) async-start(bf16[4,128,1024]{2,0,1:T(4,128)(2,1)} %bitcast.3), calls=%async_computation | async-start | bytes 2097152 | tf_op jit(solution)/shard_map/all_to_all | solution.py:22
  53.8 29.4 %all-to-all-start.1 = ((bf16[3,2,128,1024]{3,1,0,2:T(2,128)(2,1)}), bf16[3,2,128,1024]{3,1,0,2:T(2,128)(2,1)S(1)}, u32[]{:S(2)}, u32[]{:S(2)}) async-start(bf16[3,2,128,1024]{3,1,0,2:T(2,128)(2,1)} %broadcast_select_fusion), calls=%async_computation.1 | async-start | bytes 3145728 | tf_op jit(solution)/shard_map/all_to_all | solution.py:26
  87.2 4.2 %copy-start.1 = (bf16[3,512,512]{2,1,0:T(8,128)(2,1)}, bf16[3,512,512]{2,1,0:T(8,128)(2,1)S(1)}, u32[]{:S(2)}) copy-start(bf16[3,512,512]{2,1,0:T(8,128)(2,1)S(1)} %reshape.222) | copy-start | bytes 4718596
  97.5 7.9 %copy-start.3 = (bf16[3,512,512]{2,1,0:T(8,128)(2,1)S(1)}, bf16[3,512,512]{2,1,0:T(8,128)(2,1)}, u32[]{:S(2)}) copy-start(bf16[3,512,512]{2,1,0:T(8,128)(2,1)} %param.13) | copy-start | bytes 4718596
  114.4 30.1 %all-to-all-start.2 = ((bf16[3,2,128,1024]{3,1,0,2:T(2,128)(2,1)}), bf16[3,2,128,1024]{3,1,0,2:T(2,128)(2,1)}, u32[]{:S(2)}, u32[]{:S(2)}) async-start(bf16[3,2,128,1024]{3,1,0,2:T(2,128)(2,1)} %copy.48), calls=%async_computation.2 | async-start | bytes 3145728 | tf_op jit(solution)/shard_map/all_to_all | solution.py:30
  156.6 5.6 %copy-start.2 = (bf16[3,512,512]{2,1,0:T(8,128)(2,1)S(1)}, bf16[3,512,512]{2,1,0:T(8,128)(2,1)}, u32[]{:S(2)}) copy-start(bf16[3,512,512]{2,1,0:T(8,128)(2,1)} %copy-done.1) | copy-start | bytes 4718596
  156.6 24.6 %all-to-all-start.3 = ((bf16[4,128,1024]{2,0,1:T(4,128)(2,1)}), bf16[4,128,1024]{2,0,1:T(4,128)(2,1)}, u32[]{:S(2)}, u32[]{:S(2)}) async-start(bf16[4,128,1024]{2,0,1:T(4,128)(2,1)} %copy.50), calls=%async_computation.3 | async-start | bytes 2097152 | tf_op jit(solution)/shard_map/all_to_all | solution.py:34
  162.2 4.0 %copy-start.5 = (bf16[3,512,512]{2,1,0:T(8,128)(2,1)S(1)}, bf16[3,512,512]{2,1,0:T(8,128)(2,1)}, u32[]{:S(2)}) copy-start(bf16[3,512,512]{2,1,0:T(8,128)(2,1)} %param.11) | copy-start | bytes 4718596
  166.2 2.6 %copy-start.6 = (bf16[3,512,512]{2,1,0:T(8,128)(2,1)S(1)}, bf16[3,512,512]{2,1,0:T(8,128)(2,1)}, u32[]{:S(2)}) copy-start(bf16[3,512,512]{2,1,0:T(8,128)(2,1)} %param.10) | copy-start | bytes 4718596
where the time goes:
time: 184 us
  waiting for transfers between devices  72.8 us (40%)
  local copies, waits for them, and re-layouts  45.9 us (25%)
  starting transfers between devices  27.3 us (15%)
  matrix products  26.8 us (15%)
  other arithmetic  9.96 us (5%)
    all_to_all x1, waiting for transfers between devices, move_blocks(): lax.all_to_all(array, ('shard', 'tp'), split_axis=2, concat_axis=2, tiled...  24.8 us
    all_to_all x1, waiting for transfers between devices, move_updates(): lax.all_to_all(array, ('shard', 'tp'), split_axis=2, concat_axis=2, tiled...  20.3 us
    all_to_all x1, waiting for transfers between devices, move_grad(): lax.all_to_all(array, ('shard', 'tp'), split_axis=1, concat_axis=1, tiled...  17.6 us
    gather x1, local copies, waits for them, and re-layouts, shards(): picked = spread[send_local, send_row, half_index, send_tp]  13.1 us
    all_to_all x1, starting transfers between devices, move_grad(): lax.all_to_all(array, ('shard', 'tp'), split_axis=1, concat_axis=1, tiled...  11.9 us
    all_to_all x1, waiting for transfers between devices, move_stripes(): lax.all_to_all(array, ('shard', 'tp'), split_axis=1, concat_axis=1, tiled...  10.1 us
    dot_general x1, matrix products, precondition_slots(): jnp.einsum('sij,sjk->sik', left_q, scaled, preferred_element_type=jnp.flo...  7.92 us
    gather x1, local copies, waits for them, and re-layouts, shards(): gathered = returned[chosen % slots, half_grid, chosen // slots]  7.25 us
  transfers between devices with their start and end apart: 4, of which 4 were waited for; matrix products, arithmetic and copies ran while one was open for 8% of the time, Pallas kernels for 0%

commit v1 on v0

v1 whole, which is shorter than its diff:
```python
import functools

import jax
import jax.numpy as jnp
from jax import lax
from jax.experimental import pallas as pl
from jax.experimental.pallas import tpu as pltpu
from jax.sharding import PartitionSpec as P

beta_moment = 0.9
beta_second = 0.95
beta_stats = 0.95
epsilon = 1e-08

AXES = ("shard", "tp")
SUB, LANE = 8, 128
VMEM = pl.BlockSpec(memory_space=pltpu.VMEM)
SMEM = pl.BlockSpec(memory_space=pltpu.SMEM)


def exchange(array):
    return lax.all_to_all(array, AXES, split_axis=0, concat_axis=0, tiled=True)


def state_rows(table, slots):
    owners = table[:, 2]
    order = jnp.arange(owners.shape[0], dtype=jnp.int32)
    earlier = (owners[None, :] == owners[:, None]) & (order[None, :] < order[:, None])
    return owners * slots + jnp.sum(earlier.astype(jnp.int32), axis=1)


def pack_kernel(grad_ref, out_ref):
    tile_cols, tile_rows, blocks = out_ref.shape[:3]
    for j in range(blocks):
        for c in range(tile_cols):
            at = (j * tile_cols + c) * LANE
            out_ref[c, :, j] = grad_ref[:, at : at + LANE].reshape(tile_rows, SUB, LANE)


def unpack_kernel(in_ref, out_ref):
    tile_cols, tile_rows, blocks = in_ref.shape[:3]
    for j in range(blocks):
        for c in range(tile_cols):
            at = (j * tile_cols + c) * LANE
            out_ref[:, at : at + LANE] = in_ref[c, :, j].reshape(tile_rows * SUB, LANE)


def to_owner_kernel(half_step, grid_ref, slot_ref, in_ref, out_ref):
    halves = out_ref.shape[0] // 2
    out_ref[...] = jnp.zeros_like(out_ref)

    def body(n, carry):
        a = grid_ref[n]
        b = slot_ref[n] * 2
        out_ref[b] = in_ref[a]
        out_ref[b + 1] = in_ref[a + half_step]
        return carry

    lax.fori_loop(0, grid_ref.shape[0], body, 0, unroll=8)


def to_grid_kernel(half_step, grid_ref, slot_ref, in_ref, out_ref):
    def body(n, carry):
        a = grid_ref[n]
        b = slot_ref[n] * 2
        out_ref[a] = in_ref[b]
        out_ref[a + half_step] = in_ref[b + 1]
        return carry

    lax.fori_loop(0, grid_ref.shape[0], body, 0, unroll=8)


def prep_kernel(left_q_ref, right_q_ref, first_ref, left_t_ref, first_rot_ref):
    left_t = left_q_ref[0].T
    left_t_ref[0] = left_t
    part = jnp.dot(left_t, first_ref[0], preferred_element_type=jnp.float32).astype(jnp.bfloat16)
    first_rot_ref[0] = jnp.dot(part, right_q_ref[0], preferred_element_type=jnp.float32)


def slot_kernel(
    count_ref, grad_ref, left_t_ref, left_q_ref, right_q_ref, first_rot_ref, second_ref,
    block_ref, second_out_ref, result_ref,
):
    tile_cols, tile_rows, _, halves = grad_ref.shape[:4]
    high = tile_rows * SUB
    for c in range(tile_cols):
        for h in range(halves):
            block_ref[0, h * high : (h + 1) * high, c * LANE : (c + 1) * LANE] = grad_ref[
                c, :, 0, h
            ].reshape(high, LANE)
    grad = block_ref[0]
    left_grad = jnp.dot(left_t_ref[0], grad, preferred_element_type=jnp.float32).astype(jnp.bfloat16)
    rotated = jnp.dot(left_grad, right_q_ref[0], preferred_element_type=jnp.float32)
    first_rot = beta_moment * first_rot_ref[0] + (1.0 - beta_moment) * rotated
    squares = second_ref[0]
    squares_new = beta_second * squares + (1.0 - beta_second) * rotated * rotated
    kept = pl.program_id(0) < count_ref[0]
    second_out_ref[0] = jnp.where(kept, squares_new, squares)
    scaled = (first_rot / (jnp.sqrt(squares_new) + epsilon)).astype(jnp.bfloat16)
    back = jnp.dot(left_q_ref[0], scaled, preferred_element_type=jnp.float32).astype(jnp.bfloat16)
    result = lax.dot_general(
        back, right_q_ref[0], (((1,), (1,)), ((), ())), preferred_element_type=jnp.float32
    ).astype(jnp.bfloat16)
    for c in range(tile_cols):
        for h in range(halves):
            result_ref[c, :, 0, h] = result[
                h * high : (h + 1) * high, c * LANE : (c + 1) * LANE
            ].reshape(tile_rows, SUB, LANE)


def per_slot(side):
    return pl.BlockSpec((1, side, side), lambda k: (k, 0, 0))


def shards(gradient, table, left_stat, right_stat, left_basis, right_basis, moment, second):
    dev_count = lax.axis_size(AXES)
    rows, cols = gradient.shape
    slots, side, _ = left_stat.shape
    halves = side // rows
    tile_cols = side // LANE
    tile_rows = rows // SUB
    blocks = cols // side
    block_cols = lax.axis_size("tp") * blocks
    bf16, f32 = jnp.bfloat16, jnp.float32

    packed = pl.pallas_call(
        pack_kernel,
        out_shape=jax.ShapeDtypeStruct((tile_cols, tile_rows, blocks, SUB, LANE), bf16),
        in_specs=[VMEM],
        out_specs=VMEM,
    )(gradient)
    spread = exchange(packed.reshape(dev_count, blocks, SUB, LANE))

    slot_row = state_rows(table, slots)
    grid_row = table[:, 0] * (halves * block_cols) + table[:, 1]
    myself = lax.axis_index(AXES)
    count = jnp.sum((table[:, 2] == myself).astype(jnp.int32)).reshape(1)

    left_t, first_rot = pl.pallas_call(
        prep_kernel,
        grid=(slots,),
        out_shape=[
            jax.ShapeDtypeStruct((slots, side, side), bf16),
            jax.ShapeDtypeStruct((slots, side, side), f32),
        ],
        in_specs=[per_slot(side)] * 3,
        out_specs=[per_slot(side)] * 2,
        cost_estimate=pl.CostEstimate(
            flops=4 * slots * side**3, bytes_accessed=12 * slots * side**2, transcendentals=0
        ),
    )(left_basis, right_basis, moment)

    outbox = pl.pallas_call(
        functools.partial(to_owner_kernel, block_cols),
        out_shape=jax.ShapeDtypeStruct((dev_count * slots * halves, SUB, LANE), bf16),
        in_specs=[SMEM, SMEM, VMEM],
        out_specs=VMEM,
    )(grid_row, slot_row, spread.reshape(dev_count * blocks, SUB, LANE))
    inbox = exchange(outbox.reshape(dev_count, slots, halves, SUB, LANE))

    pieces = pl.BlockSpec(
        (tile_cols, tile_rows, 1, halves, SUB, LANE), lambda k: (0, 0, k, 0, 0, 0)
    )
    grad_blocks, new_second, results = pl.pallas_call(
        slot_kernel,
        grid=(slots,),
        out_shape=[
            jax.ShapeDtypeStruct((slots, side, side), bf16),
            jax.ShapeDtypeStruct((slots, side, side), f32),
            jax.ShapeDtypeStruct((tile_cols, tile_rows, slots, halves, SUB, LANE), bf16),
        ],
        in_specs=[SMEM, pieces] + [per_slot(side)] * 5,
        out_specs=[per_slot(side)] * 2 + [pieces],
        cost_estimate=pl.CostEstimate(
            flops=8 * slots * side**3, bytes_accessed=20 * slots * side**2, transcendentals=0
        ),
    )(
        count,
        inbox.reshape(tile_cols, tile_rows, slots, halves, SUB, LANE),
        left_t,
        left_basis,
        right_basis,
        first_rot,
        second,
    )
    returned = exchange(results.reshape(dev_count, slots, halves, SUB, LANE))

    kept = (jnp.arange(slots, dtype=jnp.int32) < count)[:, None, None]
    new_left = jnp.where(
        kept,
        (
            beta_stats * left_stat.astype(f32)
            + (1.0 - beta_stats)
            * jnp.einsum("sik,sjk->sij", grad_blocks, grad_blocks, preferred_element_type=f32)
        ).astype(bf16),
        left_stat,
    )
    new_right = jnp.where(
        kept,
        (
            beta_stats * right_stat.astype(f32)
            + (1.0 - beta_stats)
            * jnp.einsum("ski,skj->sij", grad_blocks, grad_blocks, preferred_element_type=f32)
        ).astype(bf16),
        right_stat,
    )
    new_moment = jnp.where(
        kept,
        (
            beta_moment * moment.astype(f32) + (1.0 - beta_moment) * grad_blocks.astype(f32)
        ).astype(bf16),
        moment,
    )

    gathered = pl.pallas_call(
        functools.partial(to_grid_kernel, block_cols),
        out_shape=jax.ShapeDtypeStruct((dev_count * blocks, SUB, LANE), bf16),
        in_specs=[SMEM, SMEM, VMEM],
        out_specs=VMEM,
    )(grid_row, slot_row, returned.reshape(dev_count * slots * halves, SUB, LANE))
    arrived = exchange(gathered.reshape(dev_count, blocks, SUB, LANE))
    update = pl.pallas_call(
        unpack_kernel,
        out_shape=jax.ShapeDtypeStruct((rows, cols), bf16),
        in_specs=[VMEM],
        out_specs=VMEM,
    )(arrived.reshape(tile_cols, tile_rows, blocks, SUB, LANE))
    return (update, new_left, new_right, new_moment, new_second)


def solution(mesh):
    states = P(AXES, None, None)
    window = P("shard", "tp")
    return jax.shard_map(
        shards,
        mesh=mesh,
        in_specs=(window, P()) + (states,) * 6,
        out_specs=(window,) + (states,) * 4,
        check_vma=False,
    )
```

time: 184 us -> 140 us (0.76)
  local copies, waits for them, and re-layouts: 45.9 us -> 4.26 us
  Pallas kernels: 0 us -> 27.4 us
  matrix products: 26.8 us -> 4.96 us
  other arithmetic: 9.96 us -> 5.95 us
  starting transfers between devices: 27.3 us -> 24.8 us
    pallas_call x0 -> x6, Pallas kernels: none -> 27.4 us  [the longest x1 10.1 us: shards(): pl.pallas_call(slot_kernel, grid=(slots,), out_shape=[jax.ShapeDtypeStruc...]
    gather x3 -> x0, local copies, waits for them, and re-layouts: 23.8 us -> none  [the longest x1 13.1 us: shards(): picked = spread[send_local, send_row, half_index, send_tp]]
    dot_general x6 -> x2, matrix products: 26.8 us -> 4.96 us  [the longest x1 2.62 us: shards(): jnp.einsum('ski,skj->sij', grad_blocks, grad_blocks, preferred_element_ty...]
    reshape x6 -> x0, local copies, waits for them, and re-layouts: 13.7 us -> none  [the longest x2 5.21 us: shards(): block_updates.reshape(slots, halves, dev_count, piece_len)]
    select_n x3 -> x1, other arithmetic: 8.92 us -> 3.46 us  [shards(): jnp.where(kept, (beta_moment * moment.astype(f32) + (1.0 - beta_moment) *...]
    all_to_all x3 -> x0, local copies, waits for them, and re-layouts: 4.99 us -> none  [the longest x1 1.86 us: move_updates(): lax.all_to_all(array, ('shard', 'tp'), split_axis=2, concat_axis=2, tiled...]
    all_to_all x4, starting transfers between devices: 27.3 us -> 24.8 us  [exchange(): return lax.all_to_all(array, AXES, split_axis=0, concat_axis=0, tiled=True)]
    unnamed x15 -> x18, local copies, waits for them, and re-layouts: 2.51 us -> 4.26 us
  transfers between devices with their start and end apart: 4 -> 4, of which waited for: 4 -> 4; matrix products, arithmetic and copies ran while one was open for 8% -> 8% of each run, Pallas kernels for 0% -> 4%
where the time goes in v1:
time: 140 us
  waiting for transfers between devices  71.4 us (51%)
  Pallas kernels  27.4 us (20%)
  starting transfers between devices  24.8 us (18%)
  other arithmetic  5.95 us (4%)
  matrix products  4.96 us (4%)
  local copies, waits for them, and re-layouts  4.26 us (3%)
    all_to_all x4, waiting for transfers between devices, exchange(): return lax.all_to_all(array, AXES, split_axis=0, concat_axis=0, tiled=True)  71.4 us
    all_to_all x4, starting transfers between devices, exchange(): return lax.all_to_all(array, AXES, split_axis=0, concat_axis=0, tiled=True)  24.8 us
    pallas_call x1, Pallas kernels, shards(): pl.pallas_call(slot_kernel, grid=(slots,), out_shape=[jax.ShapeDtypeStruc...  10.1 us
    pallas_call x1, Pallas kernels, shards(): pl.pallas_call(prep_kernel, grid=(slots,), out_shape=[jax.ShapeDtypeStruc...  6.14 us
    unnamed x18, local copies, waits for them, and re-layouts  4.26 us
    select_n x1, other arithmetic, shards(): jnp.where(kept, (beta_moment * moment.astype(f32) + (1.0 - beta_moment) *...  3.46 us
    pallas_call x1, Pallas kernels, shards(): pl.pallas_call(functools.partial(to_owner_kernel, block_cols), out_shape=...  3.23 us
    pallas_call x1, Pallas kernels, shards(): pl.pallas_call(functools.partial(to_grid_kernel, block_cols), out_shape=j...  3.04 us
  transfers between devices with their start and end apart: 4, of which 4 were waited for; matrix products, arithmetic and copies ran while one was open for 8% of the time, Pallas kernels for 4%

profile of v1, /device:TPU:1, one launch (start us, length us, event | category | flops | bytes accessed | tf_op | source)
XLA Modules:
  0.0 139.5 jit_solution(8468087341896263647)
XLA Ops:
  0.6 2.4 %shard_map.119 = bf16[4,32,4,8,128]{4,3,2,1,0:T(8,128)(2,1)} custom-call(bf16[256,2048]{1,0:T(8,128)(2,1)} %grad_ref.1), custom_call_target="tpu_custom_call" | custom-call | tf_op jit(solution)/shard_map/pallas_call | solution.py:126
  3.0 11.5 %all-to-all-start = ((bf16[128,4,8,128]{3,2,1,0:T(8,128)(2,1)}), bf16[128,4,8,128]{3,2,1,0:T(8,128)(2,1)S(1)}, u32[]{:S(2)}, u32[]{:S(2)}) async-start(bf16[128,4,8,128]{3,2,1,0:T(8,128)(2,1)} %bitcast.19), calls=%async_computation | async-start | bytes 2097152 | tf_op jit(solution)/shard_map/all_to_all | solution.py:22
  14.5 0.5 fusion.5
  15.3 1.2 fusion.4
  16.5 17.3 %all-to-all-done = bf16[128,4,8,128]{3,2,1,0:T(8,128)(2,1)S(1)} async-done(((bf16[128,4,8,128]{3,2,1,0:T(8,128)(2,1)}), bf16[128,4,8,128]{3,2,1,0:T(8,128)(2,1)S(1)}, u32[]{:S(2)}, u32[]{:S(2)}) %all-to-all-start) | async-done | bytes 1048608 | tf_op jit(solution)/shard_map/all_to_all | solution.py:22
  33.7 1.0 copy-done.2
  34.7 3.2 %shard_map.120 = bf16[768,8,128]{2,1,0:T(8,128)(2,1)} custom-call(s32[256]{0:T(256)} %bitcast.25, s32[256]{0:T(256)} %get-tuple-element.18.slot_ref, bf16[512,8,128]{2,1,0:T(8,128)(2,1)} %bitcast.18), custom_call_target="tpu_custom_call" | custom-call | tf_op jit(solution)/shard_map/pallas_call | solution.py:153
  37.9 4.4 %all-to-all-start.1 = ((bf16[128,3,2,8,128]{4,3,2,1,0:T(8,128)(2,1)}), bf16[128,3,2,8,128]{4,3,2,1,0:T(8,128)(2,1)S(1)}, u32[]{:S(2)}, u32[]{:S(2)}) async-start(bf16[128,3,2,8,128]{4,3,2,1,0:T(8,128)(2,1)} %bitcast.17), calls=%async_computation.1 | async-start | bytes 3145728 | tf_op jit(solution)/shard_map/all_to_all | solution.py:22
  42.4 6.1 %shard_map.121 = (bf16[3,512,512]{2,1,0:T(8,128)(2,1)}, f32[3,512,512]{2,1,0:T(8,128)}) custom-call(bf16[3,512,512]{2,1,0:T(8,128)(2,1)} %left_q_ref.3, bf16[3,512,512]{2,1,0:T(8,128)(2,1)} %right_q_ref.3, bf16[3,512,512]{2,1,0:T(8,128)(2,1)} %first_ref.1), custom_call_target="tpu_custom_call" | custom-call | flops 1610612736 | bytes 9437184 | tf_op jit(solution)/shard_map/pallas_call | solution.py:139
  48.5 18.8 %all-to-all-done.1 = bf16[128,3,2,8,128]{4,3,2,1,0:T(8,128)(2,1)S(1)} async-done(((bf16[128,3,2,8,128]{4,3,2,1,0:T(8,128)(2,1)}), bf16[128,3,2,8,128]{4,3,2,1,0:T(8,128)(2,1)S(1)}, u32[]{:S(2)}, u32[]{:S(2)}) %all-to-all-start.1) | async-done | bytes 1572896 | tf_op jit(solution)/shard_map/all_to_all | solution.py:22
  67.3 1.1 copy-done
  68.5 10.1 %shard_map.122 = (bf16[3,512,512]{2,1,0:T(8,128)(2,1)}, f32[3,512,512]{2,1,0:T(8,128)}, bf16[4,32,3,2,8,128]{5,4,3,2,1,0:T(8,128)(2,1)}) custom-call(s32[1]{0:T(128)} %bitcast.2.count_ref, bf16[4,32,3,2,8,128]{5,4,3,2,1,0:T(8,128)(2,1)} %bitcast.15, bf16[3,512,512]{2,1,0:T(8,128)(2,1)} %get-tuple-element.10.left_t_ref, bf16[3,512,512]{2,1,0:T(8,128)(2,1)} %left_q_ref.3, ...), custom_call_target="tpu_custom_call" | custom-call | flops 3221225472 | bytes 15728640 | tf_op jit(solution)/shard_map/pallas_call | solution.py:164
  78.6 4.4 %all-to-all-start.2 = ((bf16[128,3,2,8,128]{4,3,2,1,0:T(8,128)(2,1)}), bf16[128,3,2,8,128]{4,3,2,1,0:T(8,128)(2,1)S(1)}, u32[]{:S(2)}, u32[]{:S(2)}) async-start(bf16[128,3,2,8,128]{4,3,2,1,0:T(8,128)(2,1)} %bitcast.22), calls=%async_computation.2 | async-start | bytes 3145728 | tf_op jit(solution)/shard_map/all_to_all | solution.py:22
  83.0 0.6 iota_compare_fusion.1
  83.6 24.4 %all-to-all-done.2 = bf16[128,3,2,8,128]{4,3,2,1,0:T(8,128)(2,1)S(1)} async-done(((bf16[128,3,2,8,128]{4,3,2,1,0:T(8,128)(2,1)}), bf16[128,3,2,8,128]{4,3,2,1,0:T(8,128)(2,1)S(1)}, u32[]{:S(2)}, u32[]{:S(2)}) %all-to-all-start.2) | async-done | bytes 1572896 | tf_op jit(solution)/shard_map/all_to_all | solution.py:22
  108.0 1.1 copy-done.1
  109.1 3.0 %shard_map.123 = bf16[512,8,128]{2,1,0:T(8,128)(2,1)} custom-call(s32[256]{0:T(256)} %bitcast.26, s32[256]{0:T(256)} %get-tuple-element.18.slot_ref, bf16[768,8,128]{2,1,0:T(8,128)(2,1)} %bitcast.16), custom_call_target="tpu_custom_call" | custom-call | tf_op jit(solution)/shard_map/pallas_call | solution.py:215
  112.2 4.5 %all-to-all-start.3 = ((bf16[128,4,8,128]{3,2,1,0:T(8,128)(2,1)}), bf16[128,4,8,128]{3,2,1,0:T(8,128)(2,1)S(1)}, u32[]{:S(2)}, u32[]{:S(2)}) async-start(bf16[128,4,8,128]{3,2,1,0:T(8,128)(2,1)} %bitcast.21), calls=%async_computation.3 | async-start | bytes 2097152 | tf_op jit(solution)/shard_map/all_to_all | solution.py:22
  116.7 3.5 %fusion.2 = bf16[3,512,512]{2,1,0:T(8,128)(2,1)} fusion(bf16[3,512,512]{2,1,0:T(8,128)(2,1)S(1)} %copy-done.4, bf16[3,512,512]{2,1,0:T(8,128)(2,1)} %get-tuple-element.13, pred[3]{0:T(512)(128)(4,1)S(1)} %iota_compare_fusion.1), kind=kLoop, calls=%fused_computation.5 | loop fusion | flops 5505024 | bytes 4718595 | tf_op jit(solution)/shard_map/jit(_where)/select_n | solution.py:207
  120.2 2.6 %fusion.1 = bf16[3,512,512]{2,1,0:T(8,128)(2,1)} fusion(bf16[3,512,512]{2,1,0:T(8,128)(2,1)S(1)} %copy-done.7, bf16[3,512,512]{2,1,0:T(8,128)(2,1)S(1)} %copy-done.5, pred[3]{0:T(512)(128)(4,1)S(1)} %iota_compare_fusion.1), kind=kOutput, calls=%fused_computation.4 | convolution fusion | flops 810024960 | bytes 4718595 | tf_op jit(solution)/shard_map/ski,skj->sij/dot_general | solution.py:203
  122.8 2.3 %fusion = bf16[3,512,512]{2,1,0:T(8,128)(2,1)} fusion(bf16[3,512,512]{2,1,0:T(8,128)(2,1)S(1)} %copy-done.8, bf16[3,512,512]{2,1,0:T(8,128)(2,1)S(1)} %copy-done.5, pred[3]{0:T(512)(128)(4,1)S(1)} %iota_compare_fusion.1), kind=kOutput, calls=%fused_computation.3 | convolution fusion | flops 810024960 | bytes 4718595 | tf_op jit(solution)/shard_map/sik,sjk->sij/dot_general | solution.py:194
  125.2 10.9 %all-to-all-done.3 = bf16[128,4,8,128]{3,2,1,0:T(8,128)(2,1)S(1)} async-done(((bf16[128,4,8,128]{3,2,1,0:T(8,128)(2,1)}), bf16[128,4,8,128]{3,2,1,0:T(8,128)(2,1)S(1)}, u32[]{:S(2)}, u32[]{:S(2)}) %all-to-all-start.3) | async-done | bytes 1048608 | tf_op jit(solution)/shard_map/all_to_all | solution.py:22
  136.1 1.0 copy-done.3
  137.0 2.5 %shard_map.124 = bf16[256,2048]{1,0:T(8,128)(2,1)} custom-call(bf16[4,32,4,8,128]{4,3,2,1,0:T(8,128)(2,1)} %bitcast.20), custom_call_target="tpu_custom_call" | custom-call | tf_op jit(solution)/shard_map/pallas_call | solution.py:222
  (15 shorter events, 0.2 us)
Async XLA Ops:
  3.0 11.5 %copy-start.6 = (s32[256,3]{0,1:T(4,128)S(1)}, s32[256,3]{0,1:T(4,128)}, u32[]{:S(2)}) copy-start(s32[256,3]{0,1:T(4,128)} %param.9) | copy-start | bytes 9220
  3.0 30.7 %all-to-all-start = ((bf16[128,4,8,128]{3,2,1,0:T(8,128)(2,1)}), bf16[128,4,8,128]{3,2,1,0:T(8,128)(2,1)S(1)}, u32[]{:S(2)}, u32[]{:S(2)}) async-start(bf16[128,4,8,128]{3,2,1,0:T(8,128)(2,1)} %bitcast.19), calls=%async_computation | async-start | bytes 2097152 | tf_op jit(solution)/shard_map/all_to_all | solution.py:22
  33.7 1.0 copy-start.2
  37.9 29.4 %all-to-all-start.1 = ((bf16[128,3,2,8,128]{4,3,2,1,0:T(8,128)(2,1)}), bf16[128,3,2,8,128]{4,3,2,1,0:T(8,128)(2,1)S(1)}, u32[]{:S(2)}, u32[]{:S(2)}) async-start(bf16[128,3,2,8,128]{4,3,2,1,0:T(8,128)(2,1)} %bitcast.17), calls=%async_computation.1 | async-start | bytes 3145728 | tf_op jit(solution)/shard_map/all_to_all | solution.py:22
  67.3 1.1 copy-start
  78.6 29.4 %all-to-all-start.2 = ((bf16[128,3,2,8,128]{4,3,2,1,0:T(8,128)(2,1)}), bf16[128,3,2,8,128]{4,3,2,1,0:T(8,128)(2,1)S(1)}, u32[]{:S(2)}, u32[]{:S(2)}) async-start(bf16[128,3,2,8,128]{4,3,2,1,0:T(8,128)(2,1)} %bitcast.22), calls=%async_computation.2 | async-start | bytes 3145728 | tf_op jit(solution)/shard_map/all_to_all | solution.py:22
  108.0 1.1 copy-start.1
  112.2 4.5 %copy-start.4 = (bf16[3,512,512]{2,1,0:T(8,128)(2,1)S(1)}, bf16[3,512,512]{2,1,0:T(8,128)(2,1)}, u32[]{:S(2)}) copy-start(bf16[3,512,512]{2,1,0:T(8,128)(2,1)} %first_ref.1) | copy-start | bytes 4718596
  112.2 23.9 %all-to-all-start.3 = ((bf16[128,4,8,128]{3,2,1,0:T(8,128)(2,1)}), bf16[128,4,8,128]{3,2,1,0:T(8,128)(2,1)S(1)}, u32[]{:S(2)}, u32[]{:S(2)}) async-start(bf16[128,4,8,128]{3,2,1,0:T(8,128)(2,1)} %bitcast.21), calls=%async_computation.3 | async-start | bytes 2097152 | tf_op jit(solution)/shard_map/all_to_all | solution.py:22
  116.7 3.5 %copy-start.5 = (bf16[3,512,512]{2,1,0:T(8,128)(2,1)S(1)}, bf16[3,512,512]{2,1,0:T(8,128)(2,1)}, u32[]{:S(2)}) copy-start(bf16[3,512,512]{2,1,0:T(8,128)(2,1)} %get-tuple-element.13) | copy-start | bytes 4718596
  116.7 3.5 %copy-start.7 = (bf16[3,512,512]{2,1,0:T(8,128)(2,1)S(1)}, bf16[3,512,512]{2,1,0:T(8,128)(2,1)}, u32[]{:S(2)}) copy-start(bf16[3,512,512]{2,1,0:T(8,128)(2,1)} %param.11) | copy-start | bytes 4718596
  120.2 2.6 %copy-start.8 = (bf16[3,512,512]{2,1,0:T(8,128)(2,1)S(1)}, bf16[3,512,512]{2,1,0:T(8,128)(2,1)}, u32[]{:S(2)}) copy-start(bf16[3,512,512]{2,1,0:T(8,128)(2,1)} %param.10) | copy-start | bytes 4718596
  136.1 1.0 copy-start.3

commit v2 on v1

v2 whole, which is shorter than its diff:
```python
import functools

import jax
import jax.numpy as jnp
from jax import lax
from jax.experimental import pallas as pl
from jax.experimental.pallas import tpu as pltpu
from jax.sharding import PartitionSpec as P

beta_moment = 0.9
beta_second = 0.95
beta_stats = 0.95
epsilon = 1e-08

AXES = ("shard", "tp")
SUB, LANE = 8, 128
VMEM = pl.BlockSpec(memory_space=pltpu.VMEM)
CHUNKS = 8
SMALL = pltpu.CompilerParams(vmem_limit_bytes=8 << 20)
HBM = pl.BlockSpec(memory_space=pltpu.HBM)
SMEM = pl.BlockSpec(memory_space=pltpu.SMEM)


def exchange(array):
    return lax.all_to_all(array, AXES, split_axis=0, concat_axis=0, tiled=True)


def state_rows(table, slots):
    owners = table[:, 2]
    order = jnp.arange(owners.shape[0], dtype=jnp.int32)
    earlier = (owners[None, :] == owners[:, None]) & (order[None, :] < order[:, None])
    return owners * slots + jnp.sum(earlier.astype(jnp.int32), axis=1)


def pack_kernel(grad_ref, out_ref, held_ref, load_sems, store_sems):
    tile_cols, _, blocks = out_ref.shape[:3]
    loads, stores = [], []
    for j in range(blocks):
        for c in range(tile_cols):
            at = j * tile_cols + c
            lanes = slice(at * LANE, (at + 1) * LANE)
            loads.append(
                pltpu.make_async_copy(grad_ref.at[:, :, lanes], held_ref.at[at], load_sems.at[at])
            )
            stores.append(
                pltpu.make_async_copy(held_ref.at[at], out_ref.at[c, :, j], store_sems.at[at])
            )
            loads[-1].start()
    for load, store in zip(loads, stores):
        load.wait()
        store.start()
    for store in stores:
        store.wait()


def unpack_kernel(in_ref, out_ref, sems):
    tile_cols, _, blocks = in_ref.shape[:3]
    copies = []
    for j in range(blocks):
        for c in range(tile_cols):
            at = j * tile_cols + c
            copies.append(
                pltpu.make_async_copy(
                    in_ref.at[c, :, j], out_ref.at[:, :, at * LANE : (at + 1) * LANE], sems.at[at]
                )
            )
            copies[-1].start()
    for copy in copies:
        copy.wait()


def to_owner_kernel(half_step, cell_ref, in_ref, out_hbm, out_ref, sems):
    chunks = sems.shape[0]
    rows = cell_ref.shape[0] // chunks
    stores = []
    for r in range(chunks):
        for n in range(r * rows, (r + 1) * rows):
            a = cell_ref[n]
            out_ref[2 * n] = in_ref[a]
            out_ref[2 * n + 1] = in_ref[a + half_step]
        at = pl.ds(2 * r * rows, 2 * rows)
        stores.append(pltpu.make_async_copy(out_ref.at[at], out_hbm.at[at], sems.at[r]))
        stores[-1].start()
    for store in stores:
        store.wait()


def to_grid_kernel(half_step, row_ref, in_ref, out_hbm, out_ref, sems):
    stores = []
    for r in range(row_ref.shape[0] // half_step):
        base = r * 2 * half_step
        for c in range(half_step):
            b = row_ref[r * half_step + c] * 2
            out_ref[base + c] = in_ref[b]
            out_ref[base + c + half_step] = in_ref[b + 1]
        at = pl.ds(base, 2 * half_step)
        stores.append(pltpu.make_async_copy(out_ref.at[at], out_hbm.at[at], sems.at[r]))
        stores[-1].start()
    for store in stores:
        store.wait()


def prep_kernel(left_q_ref, right_q_ref, first_ref, left_t_ref, first_rot_ref):
    left_t = left_q_ref[0].T
    left_t_ref[0] = left_t
    part = jnp.dot(left_t, first_ref[0], preferred_element_type=jnp.float32).astype(jnp.bfloat16)
    first_rot_ref[0] = beta_moment * jnp.dot(
        part, right_q_ref[0], preferred_element_type=jnp.float32
    )


def slot_kernel(
    count_ref, grad_ref, left_t_hbm, right_q_hbm, first_rot_hbm, second_hbm, left_q_hbm,
    block_hbm, second_out_hbm, result_hbm,
    left_t_ref, right_q_ref, first_rot_ref, second_ref, left_q_ref,
    block_ref, second_out_ref, rotated_ref, result_ref,
    in_sems, block_sems, second_sems, result_sems,
):
    tile_cols, tile_rows, slots, halves = grad_ref.shape[:4]
    high = tile_rows * SUB
    inputs = (
        (left_t_hbm, left_t_ref),
        (right_q_hbm, right_q_ref),
        (first_rot_hbm, first_rot_ref),
        (second_hbm, second_ref),
        (left_q_hbm, left_q_ref),
    )
    loads = [
        [
            pltpu.make_async_copy(src.at[k], dst.at[k], in_sems.at[k, i])
            for i, (src, dst) in enumerate(inputs)
        ]
        for k in range(slots)
    ]
    for row in loads:
        for load in row:
            load.start()
    stores = []

    def store(src, dst, sem):
        stores.append(pltpu.make_async_copy(src, dst, sem))
        stores[-1].start()

    def assemble(k):
        for c in range(tile_cols):
            for h in range(halves):
                block_ref[k, h * high : (h + 1) * high, c * LANE : (c + 1) * LANE] = grad_ref[
                    c, :, k, h
                ].reshape(high, LANE)
        store(block_ref.at[k], block_hbm.at[k], block_sems.at[k])

    def rotate(k):
        left_grad = jnp.dot(left_t_ref[k], block_ref[k], preferred_element_type=jnp.float32)
        rotated_ref[k % 2] = jnp.dot(
            left_grad.astype(jnp.bfloat16), right_q_ref[k], preferred_element_type=jnp.float32
        )

    def scale(k):
        rotated = rotated_ref[k % 2]
        first_rot = first_rot_ref[k] + (1.0 - beta_moment) * rotated
        old = second_ref[k]
        squares = beta_second * old + (1.0 - beta_second) * rotated * rotated
        second_out_ref[k] = squares if k == 0 else jnp.where(k < count_ref[0], squares, old)
        root = squares * lax.rsqrt(squares)
        return (first_rot / (root + epsilon)).astype(jnp.bfloat16)

    def finish(k, scaled):
        turned = lax.dot_general(
            scaled, right_q_ref[k], (((1,), (1,)), ((), ())), preferred_element_type=jnp.float32
        ).astype(jnp.bfloat16)
        result = jnp.dot(left_q_ref[k], turned, preferred_element_type=jnp.float32).astype(
            jnp.bfloat16
        )
        for h in range(halves):
            for c in range(tile_cols):
                result_ref[c, :, k, h] = result[
                    h * high : (h + 1) * high, c * LANE : (c + 1) * LANE
                ].reshape(tile_rows, SUB, LANE)
            store(result_ref.at[:, :, k, h], result_hbm.at[:, :, k, h], result_sems.at[k, h])

    def wait(k, names):
        for i in names:
            loads[k][i].wait()

    assemble(0)
    wait(0, (0, 1))
    rotate(0)
    for k in range(slots):
        wait(k, (2, 3, 4))
        if k + 1 < slots:
            assemble(k + 1)
            wait(k + 1, (0, 1))
            rotate(k + 1)
        scaled = scale(k)
        store(second_out_ref.at[k], second_out_hbm.at[k], second_sems.at[k])
        finish(k, scaled)
    for copy in stores:
        copy.wait()


def per_slot(side):
    return pl.BlockSpec((1, side, side), lambda k: (k, 0, 0))


def near(array):
    return pltpu.with_memory_space_constraint(array, pltpu.VMEM)


def far(array):
    return pltpu.with_memory_space_constraint(array, pltpu.HBM)


def shards(gradient, table, left_stat, right_stat, left_basis, right_basis, moment, second):
    dev_count = lax.axis_size(AXES)
    rows, cols = gradient.shape
    slots, side, _ = left_stat.shape
    halves = side // rows
    tile_cols = side // LANE
    tile_rows = rows // SUB
    blocks = cols // side
    block_cols = lax.axis_size("tp") * blocks
    bf16, f32 = jnp.bfloat16, jnp.float32

    packed = pl.pallas_call(
        pack_kernel,
        out_shape=pltpu.HBM((tile_cols, tile_rows, blocks, SUB, LANE), bf16),
        in_specs=[HBM],
        out_specs=HBM,
        scratch_shapes=[
            pltpu.VMEM((blocks * tile_cols, tile_rows, SUB, LANE), bf16),
            pltpu.SemaphoreType.DMA((blocks * tile_cols,)),
            pltpu.SemaphoreType.DMA((blocks * tile_cols,)),
        ],
        compiler_params=SMALL,
    )(far(gradient.reshape(tile_rows, SUB, cols)))
    spread = exchange(packed.reshape(dev_count, blocks, SUB, LANE))

    slot_row = state_rows(table, slots)
    block_id = table[:, 0] * block_cols + table[:, 1]
    cell = block_id + table[:, 0] * ((halves - 1) * block_cols)
    targets = jnp.arange(dev_count * slots, dtype=jnp.int32)
    cell_of_row = jnp.sum(
        jnp.where(slot_row[None, :] == targets[:, None], cell[None, :], 0), axis=1
    )
    places = jnp.arange(table.shape[0], dtype=jnp.int32)
    row_of_block = jnp.sum(
        jnp.where(block_id[None, :] == places[:, None], slot_row[None, :], 0), axis=1
    )
    myself = lax.axis_index(AXES)
    count = jnp.sum((table[:, 2] == myself).astype(jnp.int32)).reshape(1)

    state = (slots, side, side)
    left_t, first_rot = pl.pallas_call(
        prep_kernel,
        grid=(slots,),
        out_shape=[jax.ShapeDtypeStruct(state, bf16), jax.ShapeDtypeStruct(state, f32)],
        in_specs=[per_slot(side)] * 3,
        out_specs=[per_slot(side)] * 2,
        cost_estimate=pl.CostEstimate(
            flops=4 * slots * side**3, bytes_accessed=12 * slots * side**2, transcendentals=0
        ),
    )(left_basis, right_basis, moment)

    outbox = pl.pallas_call(
        functools.partial(to_owner_kernel, block_cols),
        out_shape=pltpu.HBM((dev_count * slots * halves, SUB, LANE), bf16),
        in_specs=[SMEM, VMEM],
        out_specs=HBM,
        scratch_shapes=[
            pltpu.VMEM((dev_count * slots * halves, SUB, LANE), bf16),
            pltpu.SemaphoreType.DMA((CHUNKS,)),
        ],
        compiler_params=SMALL,
    )(cell_of_row, near(spread.reshape(dev_count * blocks, SUB, LANE)))
    inbox = exchange(outbox.reshape(dev_count, slots, halves, SUB, LANE))

    grad_blocks, new_second, results = pl.pallas_call(
        slot_kernel,
        out_shape=[
            jax.ShapeDtypeStruct(state, bf16),
            jax.ShapeDtypeStruct(state, f32),
            pltpu.HBM((tile_cols, tile_rows, slots, halves, SUB, LANE), bf16),
        ],
        in_specs=[SMEM, VMEM] + [HBM] * 5,
        out_specs=[HBM] * 3,
        scratch_shapes=[
            pltpu.VMEM(state, bf16),
            pltpu.VMEM(state, bf16),
            pltpu.VMEM(state, f32),
            pltpu.VMEM(state, f32),
            pltpu.VMEM(state, bf16),
            pltpu.VMEM(state, bf16),
            pltpu.VMEM(state, f32),
            pltpu.VMEM((2, side, side), f32),
            pltpu.VMEM((tile_cols, tile_rows, slots, halves, SUB, LANE), bf16),
            pltpu.SemaphoreType.DMA((slots, 5)),
            pltpu.SemaphoreType.DMA((slots,)),
            pltpu.SemaphoreType.DMA((slots,)),
            pltpu.SemaphoreType.DMA((slots, halves)),
        ],
        compiler_params=pltpu.CompilerParams(vmem_limit_bytes=48 << 20),
        cost_estimate=pl.CostEstimate(
            flops=8 * slots * side**3, bytes_accessed=20 * slots * side**2, transcendentals=0
        ),
    )(
        count,
        near(inbox.reshape(tile_cols, tile_rows, slots, halves, SUB, LANE)),
        far(left_t),
        far(right_basis),
        far(first_rot),
        far(second),
        far(left_basis),
    )
    returned = exchange(results.reshape(dev_count, slots, halves, SUB, LANE))

    kept = (jnp.arange(slots, dtype=jnp.int32) < count)[:, None, None]
    new_left = jnp.where(
        kept,
        (
            beta_stats * left_stat.astype(f32)
            + (1.0 - beta_stats)
            * jnp.einsum("sik,sjk->sij", grad_blocks, grad_blocks, preferred_element_type=f32)
        ).astype(bf16),
        left_stat,
    )
    new_right = jnp.where(
        kept,
        (
            beta_stats * right_stat.astype(f32)
            + (1.0 - beta_stats)
            * jnp.einsum("ski,skj->sij", grad_blocks, grad_blocks, preferred_element_type=f32)
        ).astype(bf16),
        right_stat,
    )
    new_moment = jnp.where(
        kept,
        (
            beta_moment * moment.astype(f32) + (1.0 - beta_moment) * grad_blocks.astype(f32)
        ).astype(bf16),
        moment,
    )

    gathered = pl.pallas_call(
        functools.partial(to_grid_kernel, block_cols),
        out_shape=pltpu.HBM((dev_count * blocks, SUB, LANE), bf16),
        in_specs=[SMEM, VMEM],
        out_specs=HBM,
        scratch_shapes=[
            pltpu.VMEM((dev_count * blocks, SUB, LANE), bf16),
            pltpu.SemaphoreType.DMA((dev_count * blocks // (halves * block_cols),)),
        ],
        compiler_params=SMALL,
    )(row_of_block, near(returned.reshape(dev_count * slots * halves, SUB, LANE)))
    arrived = exchange(gathered.reshape(dev_count, blocks, SUB, LANE))
    update = pl.pallas_call(
        unpack_kernel,
        out_shape=jax.ShapeDtypeStruct((tile_rows, SUB, cols), bf16),
        in_specs=[VMEM],
        out_specs=HBM,
        scratch_shapes=[pltpu.SemaphoreType.DMA((blocks * tile_cols,))],
        compiler_params=SMALL,
    )(near(arrived.reshape(tile_cols, tile_rows, blocks, SUB, LANE))).reshape(rows, cols)
    return (update, new_left, new_right, new_moment, new_second)


def solution(mesh):
    states = P(AXES, None, None)
    window = P("shard", "tp")
    return jax.shard_map(
        shards,
        mesh=mesh,
        in_specs=(window, P()) + (states,) * 6,
        out_specs=(window,) + (states,) * 4,
        check_vma=False,
    )
```

time: 140 us -> 129 us (0.921)
  Pallas kernels: 27.4 us -> 20.5 us
  local copies, waits for them, and re-layouts: 4.26 us -> 0.02 us
    pallas_call x4, Pallas kernels: 18 us -> 12.5 us  [the longest x1 7.67 us: shards(): pl.pallas_call(slot_kernel, out_shape=[jax.ShapeDtypeStruct(state, bf16),...]
    unnamed x18 -> x6, local copies, waits for them, and re-layouts: 4.26 us -> 0.02 us
    pallas_call x1, Pallas kernels: 3.23 us -> 1.81 us  [shards(): pl.pallas_call(functools.partial(to_owner_kernel, block_cols), out_shape=...]
  transfers between devices with their start and end apart: 4 -> 4, of which waited for: 4 -> 4; matrix products, arithmetic and copies ran while one was open for 8% -> 8% of each run, Pallas kernels for 4% -> 5%
where the time goes in v2:
time: 129 us; the launch traced here: 128 us
  waiting for transfers between devices  71.7 us (56%)
  starting transfers between devices  24.8 us (19%)
  Pallas kernels  20.5 us (16%)
  other arithmetic  5.69 us (4%)
  matrix products  4.89 us (4%)
    all_to_all x4, waiting for transfers between devices, exchange(): return lax.all_to_all(array, AXES, split_axis=0, concat_axis=0, tiled=True)  71.7 us
    all_to_all x4, starting transfers between devices, exchange(): return lax.all_to_all(array, AXES, split_axis=0, concat_axis=0, tiled=True)  24.8 us
    pallas_call x1, Pallas kernels, shards(): pl.pallas_call(slot_kernel, out_shape=[jax.ShapeDtypeStruct(state, bf16),...  7.67 us
    pallas_call x1, Pallas kernels, shards(): pl.pallas_call(prep_kernel, grid=(slots,), out_shape=[jax.ShapeDtypeStruc...  6.17 us
    select_n x1, other arithmetic, shards(): jnp.where(kept, (beta_moment * moment.astype(f32) + (1.0 - beta_moment) *...  3.96 us
  transfers between devices with their start and end apart: 4, of which 4 were waited for; matrix products, arithmetic and copies ran while one was open for 8% of the time, Pallas kernels for 5%

profile of v2, /device:TPU:1, one launch (start us, length us, event | category | flops | bytes accessed | tf_op | source)
XLA Modules:
  0.0 128.4 jit_solution(15444465905352335774)
XLA Ops:
  0.6 2.2 %shard_map.119 = bf16[4,32,4,8,128]{4,3,2,1,0:T(8,128)(2,1)} custom-call(bf16[32,8,2048]{2,1,0:T(8,128)(2,1)} %bitcast.26), custom_call_target="tpu_custom_call" | custom-call | tf_op jit(solution)/shard_map/pallas_call | solution.py:224
  2.8 0.0 copy-start
  2.8 11.5 %all-to-all-start = ((bf16[128,4,8,128]{3,2,1,0:T(8,128)(2,1)}), bf16[128,4,8,128]{3,2,1,0:T(8,128)(2,1)S(1)}, u32[]{:S(2)}, u32[]{:S(2)}) async-start(bf16[128,4,8,128]{3,2,1,0:T(8,128)(2,1)} %bitcast.24), calls=%async_computation | async-start | bytes 2097152 | tf_op jit(solution)/shard_map/all_to_all | solution.py:25
  14.4 0.2 convert_reduce_fusion
  14.5 0.6 fusion.4
  15.2 0.1 select_reduce_fusion.cell_ref
  15.3 18.2 %all-to-all-done = bf16[128,4,8,128]{3,2,1,0:T(8,128)(2,1)S(1)} async-done(((bf16[128,4,8,128]{3,2,1,0:T(8,128)(2,1)}), bf16[128,4,8,128]{3,2,1,0:T(8,128)(2,1)S(1)}, u32[]{:S(2)}, u32[]{:S(2)}) %all-to-all-start) | async-done | bytes 1048608 | tf_op jit(solution)/shard_map/all_to_all | solution.py:25
  33.6 1.8 %shard_map.120 = bf16[768,8,128]{2,1,0:T(8,128)(2,1)} custom-call(s32[384]{0:T(512)S(1)} %select_reduce_fusion.cell_ref, bf16[512,8,128]{2,1,0:T(8,128)(2,1)S(1)} %bitcast.20), custom_call_target="tpu_custom_call" | custom-call | tf_op jit(solution)/shard_map/pallas_call | solution.py:264
  35.4 4.4 %all-to-all-start.1 = ((bf16[128,3,2,8,128]{4,3,2,1,0:T(8,128)(2,1)}), bf16[128,3,2,8,128]{4,3,2,1,0:T(8,128)(2,1)S(1)}, u32[]{:S(2)}, u32[]{:S(2)}) async-start(bf16[128,3,2,8,128]{4,3,2,1,0:T(8,128)(2,1)} %bitcast.22), calls=%async_computation.1 | async-start | bytes 3145728 | tf_op jit(solution)/shard_map/all_to_all | solution.py:25
  39.8 6.2 %shard_map.121 = (bf16[3,512,512]{2,1,0:T(8,128)(2,1)}, f32[3,512,512]{2,1,0:T(8,128)}) custom-call(bf16[3,512,512]{2,1,0:T(8,128)(2,1)} %left_q_hbm.1, bf16[3,512,512]{2,1,0:T(8,128)(2,1)} %right_q_hbm.1, bf16[3,512,512]{2,1,0:T(8,128)(2,1)} %first_ref.1), custom_call_target="tpu_custom_call" | custom-call | flops 1610612736 | bytes 9437184 | tf_op jit(solution)/shard_map/pallas_call | solution.py:253
  46.0 18.8 %all-to-all-done.1 = bf16[128,3,2,8,128]{4,3,2,1,0:T(8,128)(2,1)S(1)} async-done(((bf16[128,3,2,8,128]{4,3,2,1,0:T(8,128)(2,1)}), bf16[128,3,2,8,128]{4,3,2,1,0:T(8,128)(2,1)S(1)}, u32[]{:S(2)}, u32[]{:S(2)}) %all-to-all-start.1) | async-done | bytes 1572896 | tf_op jit(solution)/shard_map/all_to_all | solution.py:25
  64.8 7.7 %shard_map.122 = (bf16[3,512,512]{2,1,0:T(8,128)(2,1)S(1)}, f32[3,512,512]{2,1,0:T(8,128)}, bf16[4,32,3,2,8,128]{5,4,3,2,1,0:T(8,128)(2,1)}) custom-call(s32[1]{0:T(128)} %bitcast.3.count_ref, bf16[4,32,3,2,8,128]{5,4,3,2,1,0:T(8,128)(2,1)S(1)} %bitcast.18, bf16[3,512,512]{2,1,0:T(8,128)(2,1)} %get-tuple-element.10.left_t_hbm, ...), custom_call_target="tpu_custom_call" | custom-call | flops 3221225472 | bytes 15728640 | tf_op jit(solution)/shard_map/pallas_call | solution.py:277
  72.5 4.4 %all-to-all-start.2 = ((bf16[128,3,2,8,128]{4,3,2,1,0:T(8,128)(2,1)}), bf16[128,3,2,8,128]{4,3,2,1,0:T(8,128)(2,1)S(1)}, u32[]{:S(2)}, u32[]{:S(2)}) async-start(bf16[128,3,2,8,128]{4,3,2,1,0:T(8,128)(2,1)} %bitcast.25), calls=%async_computation.2 | async-start | bytes 3145728 | tf_op jit(solution)/shard_map/all_to_all | solution.py:25
  76.9 0.7 iota_compare_fusion.3
  77.6 0.1 select_reduce_fusion.1.row_ref
  77.7 24.2 %all-to-all-done.2 = bf16[128,3,2,8,128]{4,3,2,1,0:T(8,128)(2,1)S(1)} async-done(((bf16[128,3,2,8,128]{4,3,2,1,0:T(8,128)(2,1)}), bf16[128,3,2,8,128]{4,3,2,1,0:T(8,128)(2,1)S(1)}, u32[]{:S(2)}, u32[]{:S(2)}) %all-to-all-start.2) | async-done | bytes 1572896 | tf_op jit(solution)/shard_map/all_to_all | solution.py:25
  101.9 1.6 %shard_map.123 = bf16[512,8,128]{2,1,0:T(8,128)(2,1)} custom-call(s32[256]{0:T(256)S(1)} %select_reduce_fusion.1.row_ref, bf16[768,8,128]{2,1,0:T(8,128)(2,1)S(1)} %bitcast.19), custom_call_target="tpu_custom_call" | custom-call | tf_op jit(solution)/shard_map/pallas_call | solution.py:343
  103.5 4.4 %all-to-all-start.3 = ((bf16[128,4,8,128]{3,2,1,0:T(8,128)(2,1)}), bf16[128,4,8,128]{3,2,1,0:T(8,128)(2,1)S(1)}, u32[]{:S(2)}, u32[]{:S(2)}) async-start(bf16[128,4,8,128]{3,2,1,0:T(8,128)(2,1)} %bitcast.23), calls=%async_computation.3 | async-start | bytes 2097152 | tf_op jit(solution)/shard_map/all_to_all | solution.py:25
  107.9 0.0 copy-start.1
  107.9 4.0 %fusion.2 = bf16[3,512,512]{2,1,0:T(8,128)(2,1)} fusion(bf16[3,512,512]{2,1,0:T(8,128)(2,1)} %first_ref.1, bf16[3,512,512]{2,1,0:T(8,128)(2,1)S(1)} %get-tuple-element.13, pred[3]{0:T(512)(128)(4,1)S(1)} %iota_compare_fusion.3), kind=kLoop, calls=%fused_computation.5 | loop fusion | flops 5505024 | bytes 4718595 | tf_op jit(solution)/shard_map/jit(_where)/select_n | solution.py:335
  111.9 2.6 %fusion.1 = bf16[3,512,512]{2,1,0:T(8,128)(2,1)} fusion(bf16[3,512,512]{2,1,0:T(8,128)(2,1)S(1)} %copy-done.1, bf16[3,512,512]{2,1,0:T(8,128)(2,1)S(1)} %get-tuple-element.13, pred[3]{0:T(512)(128)(4,1)S(1)} %iota_compare_fusion.3), kind=kOutput, calls=%fused_computation.4 | convolution fusion | flops 810024960 | bytes 4718595 | tf_op jit(solution)/shard_map/ski,skj->sij/dot_general | solution.py:331
  114.5 2.3 %fusion = bf16[3,512,512]{2,1,0:T(8,128)(2,1)} fusion(bf16[3,512,512]{2,1,0:T(8,128)(2,1)S(1)} %copy-done.2, bf16[3,512,512]{2,1,0:T(8,128)(2,1)S(1)} %get-tuple-element.13, pred[3]{0:T(512)(128)(4,1)S(1)} %iota_compare_fusion.3), kind=kOutput, calls=%fused_computation.3 | convolution fusion | flops 810024960 | bytes 4718595 | tf_op jit(solution)/shard_map/sik,sjk->sij/dot_general | solution.py:322
  116.8 10.5 %all-to-all-done.3 = bf16[128,4,8,128]{3,2,1,0:T(8,128)(2,1)S(1)} async-done(((bf16[128,4,8,128]{3,2,1,0:T(8,128)(2,1)}), bf16[128,4,8,128]{3,2,1,0:T(8,128)(2,1)S(1)}, u32[]{:S(2)}, u32[]{:S(2)}) %all-to-all-start.3) | async-done | bytes 1048608 | tf_op jit(solution)/shard_map/all_to_all | solution.py:25
  127.3 1.1 shard_map.124
  (5 shorter events, 0.0 us)
Async XLA Ops:
  2.8 11.5 %copy-start = (s32[256,3]{0,1:T(4,128)S(1)}, s32[256,3]{0,1:T(4,128)}, u32[]{:S(2)}) copy-start(s32[256,3]{0,1:T(4,128)} %param.9) | copy-start | bytes 9220
  2.8 30.7 %all-to-all-start = ((bf16[128,4,8,128]{3,2,1,0:T(8,128)(2,1)}), bf16[128,4,8,128]{3,2,1,0:T(8,128)(2,1)S(1)}, u32[]{:S(2)}, u32[]{:S(2)}) async-start(bf16[128,4,8,128]{3,2,1,0:T(8,128)(2,1)} %bitcast.24), calls=%async_computation | async-start | bytes 2097152 | tf_op jit(solution)/shard_map/all_to_all | solution.py:25
  35.4 29.4 %all-to-all-start.1 = ((bf16[128,3,2,8,128]{4,3,2,1,0:T(8,128)(2,1)}), bf16[128,3,2,8,128]{4,3,2,1,0:T(8,128)(2,1)S(1)}, u32[]{:S(2)}, u32[]{:S(2)}) async-start(bf16[128,3,2,8,128]{4,3,2,1,0:T(8,128)(2,1)} %bitcast.22), calls=%async_computation.1 | async-start | bytes 3145728 | tf_op jit(solution)/shard_map/all_to_all | solution.py:25
  72.5 29.4 %all-to-all-start.2 = ((bf16[128,3,2,8,128]{4,3,2,1,0:T(8,128)(2,1)}), bf16[128,3,2,8,128]{4,3,2,1,0:T(8,128)(2,1)S(1)}, u32[]{:S(2)}, u32[]{:S(2)}) async-start(bf16[128,3,2,8,128]{4,3,2,1,0:T(8,128)(2,1)} %bitcast.25), calls=%async_computation.2 | async-start | bytes 3145728 | tf_op jit(solution)/shard_map/all_to_all | solution.py:25
  103.5 23.8 %all-to-all-start.3 = ((bf16[128,4,8,128]{3,2,1,0:T(8,128)(2,1)}), bf16[128,4,8,128]{3,2,1,0:T(8,128)(2,1)S(1)}, u32[]{:S(2)}, u32[]{:S(2)}) async-start(bf16[128,4,8,128]{3,2,1,0:T(8,128)(2,1)} %bitcast.23), calls=%async_computation.3 | async-start | bytes 2097152 | tf_op jit(solution)/shard_map/all_to_all | solution.py:25
  107.9 4.0 %copy-start.1 = (bf16[3,512,512]{2,1,0:T(8,128)(2,1)S(1)}, bf16[3,512,512]{2,1,0:T(8,128)(2,1)}, u32[]{:S(2)}) copy-start(bf16[3,512,512]{2,1,0:T(8,128)(2,1)} %param.11) | copy-start | bytes 4718596
  111.9 2.6 %copy-start.2 = (bf16[3,512,512]{2,1,0:T(8,128)(2,1)S(1)}, bf16[3,512,512]{2,1,0:T(8,128)(2,1)}, u32[]{:S(2)}) copy-start(bf16[3,512,512]{2,1,0:T(8,128)(2,1)} %param.10) | copy-start | bytes 4718596

commit v3 on v2

--- a/solution.py
+++ b/solution.py
@@ -15,6 +15,7 @@
 AXES = ("shard", "tp")
 SUB, LANE = 8, 128
 VMEM = pl.BlockSpec(memory_space=pltpu.VMEM)
+PARTS = 4
 CHUNKS = 8
 SMALL = pltpu.CompilerParams(vmem_limit_bytes=8 << 20)
 HBM = pl.BlockSpec(memory_space=pltpu.HBM)
@@ -32,23 +33,26 @@
     return owners * slots + jnp.sum(earlier.astype(jnp.int32), axis=1)
 
 
-def pack_kernel(grad_ref, out_ref, held_ref, load_sems, store_sems):
-    tile_cols, _, blocks = out_ref.shape[:3]
+def pack_kernel(grad_ref, out_ref, held_ref, packed_ref, load_sems, store_sems):
+    tile_cols, tile_rows, blocks = out_ref.shape[:3]
+    parts = load_sems.shape[0]
+    step = tile_rows // parts
     loads, stores = [], []
-    for j in range(blocks):
-        for c in range(tile_cols):
-            at = j * tile_cols + c
-            lanes = slice(at * LANE, (at + 1) * LANE)
-            loads.append(
-                pltpu.make_async_copy(grad_ref.at[:, :, lanes], held_ref.at[at], load_sems.at[at])
-            )
-            stores.append(
-                pltpu.make_async_copy(held_ref.at[at], out_ref.at[c, :, j], store_sems.at[at])
-            )
-            loads[-1].start()
-    for load, store in zip(loads, stores):
-        load.wait()
-        store.start()
+    for r in range(parts):
+        at = pl.ds(r * step, step)
+        loads.append(pltpu.make_async_copy(grad_ref.at[at], held_ref.at[at], load_sems.at[r]))
+        stores.append(
+            pltpu.make_async_copy(packed_ref.at[:, at], out_ref.at[:, at], store_sems.at[r])
+        )
+        loads[-1].start()
+    for r in range(parts):
+        loads[r].wait()
+        rows = slice(r * step, (r + 1) * step)
+        for j in range(blocks):
+            for c in range(tile_cols):
+                at = (j * tile_cols + c) * LANE
+                packed_ref[c, rows, j] = held_ref[rows, :, at : at + LANE]
+        stores[r].start()
     for store in stores:
         store.wait()
 
@@ -100,21 +104,24 @@
         store.wait()
 
 
-def prep_kernel(left_q_ref, right_q_ref, first_ref, left_t_ref, first_rot_ref):
+def prep_kernel(
+    left_q_ref, right_q_ref, first_ref, second_ref, left_t_ref, first_rot_ref, decayed_ref
+):
     left_t = left_q_ref[0].T
     left_t_ref[0] = left_t
     part = jnp.dot(left_t, first_ref[0], preferred_element_type=jnp.float32).astype(jnp.bfloat16)
-    first_rot_ref[0] = beta_moment * jnp.dot(
+    first_rot_ref[0] = (2.0 * beta_moment) * jnp.dot(
         part, right_q_ref[0], preferred_element_type=jnp.float32
     )
+    decayed_ref[0] = (4.0 * beta_second) * second_ref[0]
 
 
 def slot_kernel(
-    count_ref, grad_ref, left_t_hbm, right_q_hbm, first_rot_hbm, second_hbm, left_q_hbm,
-    block_hbm, second_out_hbm, result_hbm,
-    left_t_ref, right_q_ref, first_rot_ref, second_ref, left_q_ref,
-    block_ref, second_out_ref, rotated_ref, result_ref,
-    in_sems, block_sems, second_sems, result_sems,
+    grad_ref, left_t_hbm, right_q_hbm, first_rot_hbm, decayed_hbm, left_q_hbm,
+    block_hbm, squares_hbm, result_hbm,
+    left_t_ref, right_q_ref, first_rot_ref, decayed_ref, left_q_ref,
+    block_ref, squares_ref, rotated_ref, result_ref,
+    in_sems, block_sems, squares_sems, result_sems,
 ):
     tile_cols, tile_rows, slots, halves = grad_ref.shape[:4]
     high = tile_rows * SUB
@@ -122,7 +129,7 @@
         (left_t_hbm, left_t_ref),
         (right_q_hbm, right_q_ref),
         (first_rot_hbm, first_rot_ref),
-        (second_hbm, second_ref),
+        (decayed_hbm, decayed_ref),
         (left_q_hbm, left_q_ref),
     )
     loads = [
@@ -142,27 +149,31 @@
         stores[-1].start()
 
     def assemble(k):
-        for c in range(tile_cols):
-            for h in range(halves):
-                block_ref[k, h * high : (h + 1) * high, c * LANE : (c + 1) * LANE] = grad_ref[
-                    c, :, k, h
-                ].reshape(high, LANE)
-        store(block_ref.at[k], block_hbm.at[k], block_sems.at[k])
+        return jnp.concatenate(
+            [
+                jnp.concatenate(
+                    [grad_ref[c, :, k, h].reshape(high, LANE) for h in range(halves)], axis=0
+                )
+                for c in range(tile_cols)
+            ],
+            axis=1,
+        )
 
     def rotate(k):
-        left_grad = jnp.dot(left_t_ref[k], block_ref[k], preferred_element_type=jnp.float32)
+        block = assemble(k)
+        block_ref[k] = block
+        left_grad = jnp.dot(left_t_ref[k], block, preferred_element_type=jnp.float32)
         rotated_ref[k % 2] = jnp.dot(
             left_grad.astype(jnp.bfloat16), right_q_ref[k], preferred_element_type=jnp.float32
         )
 
     def scale(k):
         rotated = rotated_ref[k % 2]
-        first_rot = first_rot_ref[k] + (1.0 - beta_moment) * rotated
-        old = second_ref[k]
-        squares = beta_second * old + (1.0 - beta_second) * rotated * rotated
-        second_out_ref[k] = squares if k == 0 else jnp.where(k < count_ref[0], squares, old)
+        share = (2.0 * (1.0 - beta_moment)) * rotated
+        squares = decayed_ref[k] + share * rotated
+        squares_ref[k] = squares
         root = squares * lax.rsqrt(squares)
-        return (first_rot / (root + epsilon)).astype(jnp.bfloat16)
+        return ((first_rot_ref[k] + share) / (root + 2.0 * epsilon)).astype(jnp.bfloat16)
 
     def finish(k, scaled):
         turned = lax.dot_general(
@@ -182,18 +193,21 @@
         for i in names:
             loads[k][i].wait()
 
-    assemble(0)
     wait(0, (0, 1))
     rotate(0)
     for k in range(slots):
+        last = k == slots - 1
+        store(block_ref.at[k], block_hbm.at[k], block_sems.at[k])
         wait(k, (2, 3, 4))
-        if k + 1 < slots:
-            assemble(k + 1)
+        if not last:
             wait(k + 1, (0, 1))
             rotate(k + 1)
         scaled = scale(k)
-        store(second_out_ref.at[k], second_out_hbm.at[k], second_sems.at[k])
+        if last:
+            store(squares_ref.at[k], squares_hbm.at[k], squares_sems.at[k])
         finish(k, scaled)
+        if not last:
+            store(squares_ref.at[k], squares_hbm.at[k], squares_sems.at[k])
     for copy in stores:
         copy.wait()
 
@@ -227,9 +241,10 @@
         in_specs=[HBM],
         out_specs=HBM,
         scratch_shapes=[
-            pltpu.VMEM((blocks * tile_cols, tile_rows, SUB, LANE), bf16),
-            pltpu.SemaphoreType.DMA((blocks * tile_cols,)),
-            pltpu.SemaphoreType.DMA((blocks * tile_cols,)),
+            pltpu.VMEM((tile_rows, SUB, cols), bf16),
+            pltpu.VMEM((tile_cols, tile_rows, blocks, SUB, LANE), bf16),
+            pltpu.SemaphoreType.DMA((PARTS,)),
+            pltpu.SemaphoreType.DMA((PARTS,)),
         ],
         compiler_params=SMALL,
     )(far(gradient.reshape(tile_rows, SUB, cols)))
@@ -250,16 +265,20 @@
     count = jnp.sum((table[:, 2] == myself).astype(jnp.int32)).reshape(1)
 
     state = (slots, side, side)
-    left_t, first_rot = pl.pallas_call(
+    left_t, first_rot, decayed = pl.pallas_call(
         prep_kernel,
         grid=(slots,),
-        out_shape=[jax.ShapeDtypeStruct(state, bf16), jax.ShapeDtypeStruct(state, f32)],
-        in_specs=[per_slot(side)] * 3,
-        out_specs=[per_slot(side)] * 2,
+        out_shape=[
+            jax.ShapeDtypeStruct(state, bf16),
+            jax.ShapeDtypeStruct(state, f32),
+            jax.ShapeDtypeStruct(state, f32),
+        ],
+        in_specs=[per_slot(side)] * 4,
+        out_specs=[per_slot(side)] * 3,
         cost_estimate=pl.CostEstimate(
-            flops=4 * slots * side**3, bytes_accessed=12 * slots * side**2, transcendentals=0
+            flops=4 * slots * side**3, bytes_accessed=20 * slots * side**2, transcendentals=0
         ),
-    )(left_basis, right_basis, moment)
+    )(left_basis, right_basis, moment, second)
 
     outbox = pl.pallas_call(
         functools.partial(to_owner_kernel, block_cols),
@@ -274,14 +293,14 @@
     )(cell_of_row, near(spread.reshape(dev_count * blocks, SUB, LANE)))
     inbox = exchange(outbox.reshape(dev_count, slots, halves, SUB, LANE))
 
-    grad_blocks, new_second, results = pl.pallas_call(
+    grad_blocks, squares, results = pl.pallas_call(
         slot_kernel,
         out_shape=[
             jax.ShapeDtypeStruct(state, bf16),
             jax.ShapeDtypeStruct(state, f32),
             pltpu.HBM((tile_cols, tile_rows, slots, halves, SUB, LANE), bf16),
         ],
-        in_specs=[SMEM, VMEM] + [HBM] * 5,
+        in_specs=[VMEM] + [HBM] * 5,
         out_specs=[HBM] * 3,
         scratch_shapes=[
             pltpu.VMEM(state, bf16),
@@ -303,12 +322,11 @@
             flops=8 * slots * side**3, bytes_accessed=20 * slots * side**2, transcendentals=0
         ),
     )(
-        count,
         near(inbox.reshape(tile_cols, tile_rows, slots, halves, SUB, LANE)),
         far(left_t),
         far(right_basis),
         far(first_rot),
-        far(second),
+        far(decayed),
         far(left_basis),
     )
     returned = exchange(results.reshape(dev_count, slots, halves, SUB, LANE))
@@ -332,6 +350,7 @@
         ).astype(bf16),
         right_stat,
     )
+    new_second = jnp.where(kept, 0.25 * squares, second)
     new_moment = jnp.where(
         kept,
         (

time: 129 us -> 128 us (level)
  waiting for transfers between devices: 71.7 us -> 63.4 us
  other arithmetic: 5.69 us -> 10.3 us
  matrix products: 4.89 us -> 6.84 us
    all_to_all x4, waiting for transfers between devices: 71.7 us -> 63.4 us  [exchange(): return lax.all_to_all(array, AXES, split_axis=0, concat_axis=0, tiled=True)]
    select_n x0 -> x1, other arithmetic: none -> 4.53 us  [shards(): new_second = jnp.where(kept, 0.25 * squares, second)]
    dot_general x1, matrix products: 2.57 us -> 4.53 us  [shards(): jnp.einsum('ski,skj->sij', grad_blocks, grad_blocks, preferred_element_ty...]
    pallas_call x1, Pallas kernels: 6.17 us -> 7.94 us  [shards(): pl.pallas_call(prep_kernel, grid=(slots,), out_shape=[jax.ShapeDtypeStruc...]
  transfers between devices with their start and end apart: 4 -> 4, of which waited for: 4 -> 4; matrix products, arithmetic and copies ran while one was open for 8% -> 13% of each run, Pallas kernels for 5% -> 6%
where the time goes in v3:
time: 128 us
  waiting for transfers between devices  63.4 us (50%)
  starting transfers between devices  24.8 us (19%)
  Pallas kernels  21.4 us (17%)
  other arithmetic  10.3 us (8%)
  matrix products  6.84 us (5%)
    all_to_all x4, waiting for transfers between devices, exchange(): return lax.all_to_all(array, AXES, split_axis=0, concat_axis=0, tiled=True)  63.4 us
    all_to_all x4, starting transfers between devices, exchange(): return lax.all_to_all(array, AXES, split_axis=0, concat_axis=0, tiled=True)  24.8 us
    pallas_call x1, Pallas kernels, shards(): pl.pallas_call(prep_kernel, grid=(slots,), out_shape=[jax.ShapeDtypeStruc...  7.94 us
    pallas_call x1, Pallas kernels, shards(): pl.pallas_call(slot_kernel, out_shape=[jax.ShapeDtypeStruct(state, bf16),...  6.9 us
    select_n x1, other arithmetic, shards(): new_second = jnp.where(kept, 0.25 * squares, second)  4.53 us
    dot_general x1, matrix products, shards(): jnp.einsum('ski,skj->sij', grad_blocks, grad_blocks, preferred_element_ty...  4.53 us
    select_n x1, other arithmetic, shards(): jnp.where(kept, (beta_moment * moment.astype(f32) + (1.0 - beta_moment) *...  3.99 us
  transfers between devices with their start and end apart: 4, of which 4 were waited for; matrix products, arithmetic and copies ran while one was open for 13% of the time, Pallas kernels for 6%

profile of v3, /device:TPU:1, one launch (start us, length us, event | category | flops | bytes accessed | tf_op | source)
XLA Modules:
  0.0 127.6 jit_solution(1230027418977841047)
XLA Ops:
  0.6 2.0 %shard_map.119 = bf16[4,32,4,8,128]{4,3,2,1,0:T(8,128)(2,1)} custom-call(bf16[32,8,2048]{2,1,0:T(8,128)(2,1)} %bitcast.25), custom_call_target="tpu_custom_call" | custom-call | tf_op jit(solution)/shard_map/pallas_call | solution.py:238
  2.7 0.0 copy-start.1
  2.7 11.5 %all-to-all-start = ((bf16[128,4,8,128]{3,2,1,0:T(8,128)(2,1)}), bf16[128,4,8,128]{3,2,1,0:T(8,128)(2,1)S(1)}, u32[]{:S(2)}, u32[]{:S(2)}) async-start(bf16[128,4,8,128]{3,2,1,0:T(8,128)(2,1)} %bitcast.23), calls=%async_computation | async-start | bytes 2097152 | tf_op jit(solution)/shard_map/all_to_all | solution.py:26
  14.2 0.2 convert_reduce_fusion
  14.4 0.6 fusion.4
  15.0 0.1 select_reduce_fusion.cell_ref
  15.2 18.2 %all-to-all-done = bf16[128,4,8,128]{3,2,1,0:T(8,128)(2,1)S(1)} async-done(((bf16[128,4,8,128]{3,2,1,0:T(8,128)(2,1)}), bf16[128,4,8,128]{3,2,1,0:T(8,128)(2,1)S(1)}, u32[]{:S(2)}, u32[]{:S(2)}) %all-to-all-start) | async-done | bytes 1048608 | tf_op jit(solution)/shard_map/all_to_all | solution.py:26
  33.4 1.8 %shard_map.120 = bf16[768,8,128]{2,1,0:T(8,128)(2,1)} custom-call(s32[384]{0:T(512)S(1)} %select_reduce_fusion.cell_ref, bf16[512,8,128]{2,1,0:T(8,128)(2,1)S(1)} %bitcast.19), custom_call_target="tpu_custom_call" | custom-call | tf_op jit(solution)/shard_map/pallas_call | solution.py:283
  35.2 4.4 %all-to-all-start.1 = ((bf16[128,3,2,8,128]{4,3,2,1,0:T(8,128)(2,1)}), bf16[128,3,2,8,128]{4,3,2,1,0:T(8,128)(2,1)S(1)}, u32[]{:S(2)}, u32[]{:S(2)}) async-start(bf16[128,3,2,8,128]{4,3,2,1,0:T(8,128)(2,1)} %bitcast.21), calls=%async_computation.1 | async-start | bytes 3145728 | tf_op jit(solution)/shard_map/all_to_all | solution.py:26
  39.7 7.9 %shard_map.121 = (bf16[3,512,512]{2,1,0:T(8,128)(2,1)}, f32[3,512,512]{2,1,0:T(8,128)}, f32[3,512,512]{2,1,0:T(8,128)}) custom-call(bf16[3,512,512]{2,1,0:T(8,128)(2,1)} %left_q_hbm.1, bf16[3,512,512]{2,1,0:T(8,128)(2,1)} %right_q_hbm.1, bf16[3,512,512]{2,1,0:T(8,128)(2,1)} %first_ref.1, f32[3,512,512]{2,1,0:T(8,128)} %second_ref.1), custom_call_target="tpu_custom_call" | custom-call | flops 1610612736 | bytes 15728640 | tf_op jit(solution)/shard_map/pallas_call | solution.py:268
  47.6 17.0 %all-to-all-done.1 = bf16[128,3,2,8,128]{4,3,2,1,0:T(8,128)(2,1)S(1)} async-done(((bf16[128,3,2,8,128]{4,3,2,1,0:T(8,128)(2,1)}), bf16[128,3,2,8,128]{4,3,2,1,0:T(8,128)(2,1)S(1)}, u32[]{:S(2)}, u32[]{:S(2)}) %all-to-all-start.1) | async-done | bytes 1572896 | tf_op jit(solution)/shard_map/all_to_all | solution.py:26
  64.6 6.9 %shard_map.122 = (bf16[3,512,512]{2,1,0:T(8,128)(2,1)S(1)}, f32[3,512,512]{2,1,0:T(8,128)}, bf16[4,32,3,2,8,128]{5,4,3,2,1,0:T(8,128)(2,1)}) custom-call(bf16[4,32,3,2,8,128]{5,4,3,2,1,0:T(8,128)(2,1)S(1)} %bitcast.17, bf16[3,512,512]{2,1,0:T(8,128)(2,1)} %get-tuple-element.11.left_t_hbm, bf16[3,512,512]{2,1,0:T(8,128)(2,1)} %right_q_hbm.1, ...), custom_call_target="tpu_custom_call" | custom-call | flops 3221225472 | bytes 15728640 | tf_op jit(solution)/shard_map/pallas_call | solution.py:296
  71.5 4.4 %all-to-all-start.2 = ((bf16[128,3,2,8,128]{4,3,2,1,0:T(8,128)(2,1)}), bf16[128,3,2,8,128]{4,3,2,1,0:T(8,128)(2,1)S(1)}, u32[]{:S(2)}, u32[]{:S(2)}) async-start(bf16[128,3,2,8,128]{4,3,2,1,0:T(8,128)(2,1)} %bitcast.24), calls=%async_computation.2 | async-start | bytes 3145728 | tf_op jit(solution)/shard_map/all_to_all | solution.py:26
  76.0 0.7 iota_compare_fusion.3
  76.6 0.1 select_reduce_fusion.1.row_ref
  76.7 4.5 %fusion.1 = bf16[3,512,512]{2,1,0:T(8,128)(2,1)} fusion(bf16[3,512,512]{2,1,0:T(8,128)(2,1)} %param.11, bf16[3,512,512]{2,1,0:T(8,128)(2,1)S(1)} %get-tuple-element.15, pred[3]{0:T(512)(128)(4,1)S(1)} %iota_compare_fusion.3), kind=kOutput, calls=%fused_computation.5 | convolution fusion | flops 810024960 | bytes 4718595 | tf_op jit(solution)/shard_map/ski,skj->sij/dot_general | solution.py:349
  81.3 19.7 %all-to-all-done.2 = bf16[128,3,2,8,128]{4,3,2,1,0:T(8,128)(2,1)S(1)} async-done(((bf16[128,3,2,8,128]{4,3,2,1,0:T(8,128)(2,1)}), bf16[128,3,2,8,128]{4,3,2,1,0:T(8,128)(2,1)S(1)}, u32[]{:S(2)}, u32[]{:S(2)}) %all-to-all-start.2) | async-done | bytes 1572896 | tf_op jit(solution)/shard_map/all_to_all | solution.py:26
  100.9 1.6 %shard_map.123 = bf16[512,8,128]{2,1,0:T(8,128)(2,1)} custom-call(s32[256]{0:T(256)S(1)} %select_reduce_fusion.1.row_ref, bf16[768,8,128]{2,1,0:T(8,128)(2,1)S(1)} %bitcast.18), custom_call_target="tpu_custom_call" | custom-call | tf_op jit(solution)/shard_map/pallas_call | solution.py:362
  102.6 4.4 %all-to-all-start.3 = ((bf16[128,4,8,128]{3,2,1,0:T(8,128)(2,1)}), bf16[128,4,8,128]{3,2,1,0:T(8,128)(2,1)S(1)}, u32[]{:S(2)}, u32[]{:S(2)}) async-start(bf16[128,4,8,128]{3,2,1,0:T(8,128)(2,1)} %bitcast.22), calls=%async_computation.3 | async-start | bytes 2097152 | tf_op jit(solution)/shard_map/all_to_all | solution.py:26
  107.0 4.0 %fusion.2 = bf16[3,512,512]{2,1,0:T(8,128)(2,1)} fusion(bf16[3,512,512]{2,1,0:T(8,128)(2,1)} %first_ref.1, bf16[3,512,512]{2,1,0:T(8,128)(2,1)S(1)} %get-tuple-element.15, pred[3]{0:T(512)(128)(4,1)S(1)} %iota_compare_fusion.3), kind=kLoop, calls=%fused_computation.6 | loop fusion | flops 5505024 | bytes 4718595 | tf_op jit(solution)/shard_map/jit(_where)/select_n | solution.py:354
  111.0 4.5 %multiply_select_fusion = f32[3,512,512]{2,1,0:T(8,128)} fusion(f32[3,512,512]{2,1,0:T(8,128)S(1)} %copy-done, f32[3,512,512]{2,1,0:T(8,128)} %get-tuple-element.16, pred[3]{0:T(512)(128)(4,1)S(1)} %iota_compare_fusion.3), kind=kLoop, calls=%fused_computation | loop fusion | flops 1572864 | bytes 9437187 | tf_op jit(solution)/shard_map/jit(_where)/select_n | solution.py:353
  115.5 2.3 %fusion = bf16[3,512,512]{2,1,0:T(8,128)(2,1)} fusion(bf16[3,512,512]{2,1,0:T(8,128)(2,1)S(1)} %copy-done.2, bf16[3,512,512]{2,1,0:T(8,128)(2,1)S(1)} %get-tuple-element.15, pred[3]{0:T(512)(128)(4,1)S(1)} %iota_compare_fusion.3), kind=kOutput, calls=%fused_computation.4 | convolution fusion | flops 810024960 | bytes 4718595 | tf_op jit(solution)/shard_map/sik,sjk->sij/dot_general | solution.py:340
  117.8 8.5 %all-to-all-done.3 = bf16[128,4,8,128]{3,2,1,0:T(8,128)(2,1)S(1)} async-done(((bf16[128,4,8,128]{3,2,1,0:T(8,128)(2,1)}), bf16[128,4,8,128]{3,2,1,0:T(8,128)(2,1)S(1)}, u32[]{:S(2)}, u32[]{:S(2)}) %all-to-all-start.3) | async-done | bytes 1048608 | tf_op jit(solution)/shard_map/all_to_all | solution.py:26
  126.3 1.1 shard_map.124
  (6 shorter events, 0.0 us)
Async XLA Ops:
  2.7 11.5 %copy-start.1 = (s32[256,3]{0,1:T(4,128)S(1)}, s32[256,3]{0,1:T(4,128)}, u32[]{:S(2)}) copy-start(s32[256,3]{0,1:T(4,128)} %param.9) | copy-start | bytes 9220
  2.7 30.7 %all-to-all-start = ((bf16[128,4,8,128]{3,2,1,0:T(8,128)(2,1)}), bf16[128,4,8,128]{3,2,1,0:T(8,128)(2,1)S(1)}, u32[]{:S(2)}, u32[]{:S(2)}) async-start(bf16[128,4,8,128]{3,2,1,0:T(8,128)(2,1)} %bitcast.23), calls=%async_computation | async-start | bytes 2097152 | tf_op jit(solution)/shard_map/all_to_all | solution.py:26
  35.2 29.4 %all-to-all-start.1 = ((bf16[128,3,2,8,128]{4,3,2,1,0:T(8,128)(2,1)}), bf16[128,3,2,8,128]{4,3,2,1,0:T(8,128)(2,1)S(1)}, u32[]{:S(2)}, u32[]{:S(2)}) async-start(bf16[128,3,2,8,128]{4,3,2,1,0:T(8,128)(2,1)} %bitcast.21), calls=%async_computation.1 | async-start | bytes 3145728 | tf_op jit(solution)/shard_map/all_to_all | solution.py:26
  71.5 29.4 %all-to-all-start.2 = ((bf16[128,3,2,8,128]{4,3,2,1,0:T(8,128)(2,1)}), bf16[128,3,2,8,128]{4,3,2,1,0:T(8,128)(2,1)S(1)}, u32[]{:S(2)}, u32[]{:S(2)}) async-start(bf16[128,3,2,8,128]{4,3,2,1,0:T(8,128)(2,1)} %bitcast.24), calls=%async_computation.2 | async-start | bytes 3145728 | tf_op jit(solution)/shard_map/all_to_all | solution.py:26
  102.6 23.8 %all-to-all-start.3 = ((bf16[128,4,8,128]{3,2,1,0:T(8,128)(2,1)}), bf16[128,4,8,128]{3,2,1,0:T(8,128)(2,1)S(1)}, u32[]{:S(2)}, u32[]{:S(2)}) async-start(bf16[128,4,8,128]{3,2,1,0:T(8,128)(2,1)} %bitcast.22), calls=%async_computation.3 | async-start | bytes 2097152 | tf_op jit(solution)/shard_map/all_to_all | solution.py:26
  107.0 4.0 %copy-start = (f32[3,512,512]{2,1,0:T(8,128)S(1)}, f32[3,512,512]{2,1,0:T(8,128)}, u32[]{:S(2)}) copy-start(f32[3,512,512]{2,1,0:T(8,128)} %second_ref.1) | copy-start | bytes 9437188
  111.0 4.5 %copy-start.2 = (bf16[3,512,512]{2,1,0:T(8,128)(2,1)S(1)}, bf16[3,512,512]{2,1,0:T(8,128)(2,1)}, u32[]{:S(2)}) copy-start(bf16[3,512,512]{2,1,0:T(8,128)(2,1)} %param.10) | copy-start | bytes 4718596

commit v4 on v3

--- a/solution.py
+++ b/solution.py
@@ -163,6 +163,8 @@
         block = assemble(k)
         block_ref[k] = block
         left_grad = jnp.dot(left_t_ref[k], block, preferred_element_type=jnp.float32)
+        if k == 0:
+            wait(0, (1,))
         rotated_ref[k % 2] = jnp.dot(
             left_grad.astype(jnp.bfloat16), right_q_ref[k], preferred_element_type=jnp.float32
         )
@@ -179,21 +181,26 @@
         turned = lax.dot_general(
             scaled, right_q_ref[k], (((1,), (1,)), ((), ())), preferred_element_type=jnp.float32
         ).astype(jnp.bfloat16)
-        result = jnp.dot(left_q_ref[k], turned, preferred_element_type=jnp.float32).astype(
-            jnp.bfloat16
-        )
-        for h in range(halves):
-            for c in range(tile_cols):
-                result_ref[c, :, k, h] = result[
-                    h * high : (h + 1) * high, c * LANE : (c + 1) * LANE
-                ].reshape(tile_rows, SUB, LANE)
-            store(result_ref.at[:, :, k, h], result_hbm.at[:, :, k, h], result_sems.at[k, h])
+        turns = halves if k == slots - 1 else 1
+        for part in range(turns):
+            size = halves // turns
+            rows = slice(part * size * high, (part + 1) * size * high)
+            result = jnp.dot(
+                left_q_ref[k, rows], turned, preferred_element_type=jnp.float32
+            ).astype(jnp.bfloat16)
+            for n in range(size):
+                h = part * size + n
+                for c in range(tile_cols):
+                    result_ref[c, :, k, h] = result[
+                        n * high : (n + 1) * high, c * LANE : (c + 1) * LANE
+                    ].reshape(tile_rows, SUB, LANE)
+                store(result_ref.at[:, :, k, h], result_hbm.at[:, :, k, h], result_sems.at[k, h])
 
     def wait(k, names):
         for i in names:
             loads[k][i].wait()
 
-    wait(0, (0, 1))
+    wait(0, (0,))
     rotate(0)
     for k in range(slots):
         last = k == slots - 1

time: 128 us -> 128 us (level)
  no operation moved by 1% of the time
where the time goes in v4:
time: 128 us
  waiting for transfers between devices  63.5 us (50%)
  starting transfers between devices  24.8 us (19%)
  Pallas kernels  21.4 us (17%)
  other arithmetic  10.3 us (8%)
  matrix products  6.83 us (5%)
    all_to_all x4, waiting for transfers between devices, exchange(): return lax.all_to_all(array, AXES, split_axis=0, concat_axis=0, tiled=True)  63.5 us
    all_to_all x4, starting transfers between devices, exchange(): return lax.all_to_all(array, AXES, split_axis=0, concat_axis=0, tiled=True)  24.8 us
    pallas_call x1, Pallas kernels, shards(): pl.pallas_call(prep_kernel, grid=(slots,), out_shape=[jax.ShapeDtypeStruc...  7.94 us
    pallas_call x1, Pallas kernels, shards(): pl.pallas_call(slot_kernel, out_shape=[jax.ShapeDtypeStruct(state, bf16),...  6.89 us
    dot_general x1, matrix products, shards(): jnp.einsum('ski,skj->sij', grad_blocks, grad_blocks, preferred_element_ty...  4.53 us
    select_n x1, other arithmetic, shards(): new_second = jnp.where(kept, 0.25 * squares, second)  4.53 us
    select_n x1, other arithmetic, shards(): jnp.where(kept, (beta_moment * moment.astype(f32) + (1.0 - beta_moment) *...  3.99 us
  transfers between devices with their start and end apart: 4, of which 4 were waited for; matrix products, arithmetic and copies ran while one was open for 13% of the time, Pallas kernels for 6%

profile of v4, /device:TPU:1, one launch (start us, length us, event | category | flops | bytes accessed | tf_op | source)
XLA Modules:
  0.0 127.6 jit_solution(12540497008858342071)
XLA Ops:
  0.6 2.0 %shard_map.119 = bf16[4,32,4,8,128]{4,3,2,1,0:T(8,128)(2,1)} custom-call(bf16[32,8,2048]{2,1,0:T(8,128)(2,1)} %bitcast.25), custom_call_target="tpu_custom_call" | custom-call | tf_op jit(solution)/shard_map/pallas_call | solution.py:245
  2.7 0.0 copy-start.1
  2.7 11.5 %all-to-all-start = ((bf16[128,4,8,128]{3,2,1,0:T(8,128)(2,1)}), bf16[128,4,8,128]{3,2,1,0:T(8,128)(2,1)S(1)}, u32[]{:S(2)}, u32[]{:S(2)}) async-start(bf16[128,4,8,128]{3,2,1,0:T(8,128)(2,1)} %bitcast.23), calls=%async_computation | async-start | bytes 2097152 | tf_op jit(solution)/shard_map/all_to_all | solution.py:26
  14.2 0.2 convert_reduce_fusion
  14.4 0.6 fusion.4
  15.0 0.1 select_reduce_fusion.cell_ref
  15.2 18.2 %all-to-all-done = bf16[128,4,8,128]{3,2,1,0:T(8,128)(2,1)S(1)} async-done(((bf16[128,4,8,128]{3,2,1,0:T(8,128)(2,1)}), bf16[128,4,8,128]{3,2,1,0:T(8,128)(2,1)S(1)}, u32[]{:S(2)}, u32[]{:S(2)}) %all-to-all-start) | async-done | bytes 1048608 | tf_op jit(solution)/shard_map/all_to_all | solution.py:26
  33.4 1.8 %shard_map.120 = bf16[768,8,128]{2,1,0:T(8,128)(2,1)} custom-call(s32[384]{0:T(512)S(1)} %select_reduce_fusion.cell_ref, bf16[512,8,128]{2,1,0:T(8,128)(2,1)S(1)} %bitcast.19), custom_call_target="tpu_custom_call" | custom-call | tf_op jit(solution)/shard_map/pallas_call | solution.py:290
  35.2 4.4 %all-to-all-start.1 = ((bf16[128,3,2,8,128]{4,3,2,1,0:T(8,128)(2,1)}), bf16[128,3,2,8,128]{4,3,2,1,0:T(8,128)(2,1)S(1)}, u32[]{:S(2)}, u32[]{:S(2)}) async-start(bf16[128,3,2,8,128]{4,3,2,1,0:T(8,128)(2,1)} %bitcast.21), calls=%async_computation.1 | async-start | bytes 3145728 | tf_op jit(solution)/shard_map/all_to_all | solution.py:26
  39.7 7.9 %shard_map.121 = (bf16[3,512,512]{2,1,0:T(8,128)(2,1)}, f32[3,512,512]{2,1,0:T(8,128)}, f32[3,512,512]{2,1,0:T(8,128)}) custom-call(bf16[3,512,512]{2,1,0:T(8,128)(2,1)} %left_q_hbm.1, bf16[3,512,512]{2,1,0:T(8,128)(2,1)} %right_q_hbm.1, bf16[3,512,512]{2,1,0:T(8,128)(2,1)} %first_ref.1, f32[3,512,512]{2,1,0:T(8,128)} %second_ref.1), custom_call_target="tpu_custom_call" | custom-call | flops 1610612736 | bytes 15728640 | tf_op jit(solution)/shard_map/pallas_call | solution.py:275
  47.6 17.0 %all-to-all-done.1 = bf16[128,3,2,8,128]{4,3,2,1,0:T(8,128)(2,1)S(1)} async-done(((bf16[128,3,2,8,128]{4,3,2,1,0:T(8,128)(2,1)}), bf16[128,3,2,8,128]{4,3,2,1,0:T(8,128)(2,1)S(1)}, u32[]{:S(2)}, u32[]{:S(2)}) %all-to-all-start.1) | async-done | bytes 1572896 | tf_op jit(solution)/shard_map/all_to_all | solution.py:26
  64.6 6.9 %shard_map.122 = (bf16[3,512,512]{2,1,0:T(8,128)(2,1)S(1)}, f32[3,512,512]{2,1,0:T(8,128)}, bf16[4,32,3,2,8,128]{5,4,3,2,1,0:T(8,128)(2,1)}) custom-call(bf16[4,32,3,2,8,128]{5,4,3,2,1,0:T(8,128)(2,1)S(1)} %bitcast.17, bf16[3,512,512]{2,1,0:T(8,128)(2,1)} %get-tuple-element.11.left_t_hbm, bf16[3,512,512]{2,1,0:T(8,128)(2,1)} %right_q_hbm.1, ...), custom_call_target="tpu_custom_call" | custom-call | flops 3221225472 | bytes 15728640 | tf_op jit(solution)/shard_map/pallas_call | solution.py:303
  71.5 4.4 %all-to-all-start.2 = ((bf16[128,3,2,8,128]{4,3,2,1,0:T(8,128)(2,1)}), bf16[128,3,2,8,128]{4,3,2,1,0:T(8,128)(2,1)S(1)}, u32[]{:S(2)}, u32[]{:S(2)}) async-start(bf16[128,3,2,8,128]{4,3,2,1,0:T(8,128)(2,1)} %bitcast.24), calls=%async_computation.2 | async-start | bytes 3145728 | tf_op jit(solution)/shard_map/all_to_all | solution.py:26
  75.9 0.7 iota_compare_fusion.3
  76.6 0.1 select_reduce_fusion.1.row_ref
  76.7 4.5 %fusion.1 = bf16[3,512,512]{2,1,0:T(8,128)(2,1)} fusion(bf16[3,512,512]{2,1,0:T(8,128)(2,1)} %param.11, bf16[3,512,512]{2,1,0:T(8,128)(2,1)S(1)} %get-tuple-element.15, pred[3]{0:T(512)(128)(4,1)S(1)} %iota_compare_fusion.3), kind=kOutput, calls=%fused_computation.5 | convolution fusion | flops 810024960 | bytes 4718595 | tf_op jit(solution)/shard_map/ski,skj->sij/dot_general | solution.py:356
  81.3 19.7 %all-to-all-done.2 = bf16[128,3,2,8,128]{4,3,2,1,0:T(8,128)(2,1)S(1)} async-done(((bf16[128,3,2,8,128]{4,3,2,1,0:T(8,128)(2,1)}), bf16[128,3,2,8,128]{4,3,2,1,0:T(8,128)(2,1)S(1)}, u32[]{:S(2)}, u32[]{:S(2)}) %all-to-all-start.2) | async-done | bytes 1572896 | tf_op jit(solution)/shard_map/all_to_all | solution.py:26
  100.9 1.6 %shard_map.123 = bf16[512,8,128]{2,1,0:T(8,128)(2,1)} custom-call(s32[256]{0:T(256)S(1)} %select_reduce_fusion.1.row_ref, bf16[768,8,128]{2,1,0:T(8,128)(2,1)S(1)} %bitcast.18), custom_call_target="tpu_custom_call" | custom-call | tf_op jit(solution)/shard_map/pallas_call | solution.py:369
  102.6 4.4 %all-to-all-start.3 = ((bf16[128,4,8,128]{3,2,1,0:T(8,128)(2,1)}), bf16[128,4,8,128]{3,2,1,0:T(8,128)(2,1)S(1)}, u32[]{:S(2)}, u32[]{:S(2)}) async-start(bf16[128,4,8,128]{3,2,1,0:T(8,128)(2,1)} %bitcast.22), calls=%async_computation.3 | async-start | bytes 2097152 | tf_op jit(solution)/shard_map/all_to_all | solution.py:26
  107.0 4.0 %fusion.2 = bf16[3,512,512]{2,1,0:T(8,128)(2,1)} fusion(bf16[3,512,512]{2,1,0:T(8,128)(2,1)} %first_ref.1, bf16[3,512,512]{2,1,0:T(8,128)(2,1)S(1)} %get-tuple-element.15, pred[3]{0:T(512)(128)(4,1)S(1)} %iota_compare_fusion.3), kind=kLoop, calls=%fused_computation.6 | loop fusion | flops 5505024 | bytes 4718595 | tf_op jit(solution)/shard_map/jit(_where)/select_n | solution.py:361
  111.0 4.5 %multiply_select_fusion = f32[3,512,512]{2,1,0:T(8,128)} fusion(f32[3,512,512]{2,1,0:T(8,128)S(1)} %copy-done, f32[3,512,512]{2,1,0:T(8,128)} %get-tuple-element.16, pred[3]{0:T(512)(128)(4,1)S(1)} %iota_compare_fusion.3), kind=kLoop, calls=%fused_computation | loop fusion | flops 1572864 | bytes 9437187 | tf_op jit(solution)/shard_map/jit(_where)/select_n | solution.py:360
  115.5 2.3 %fusion = bf16[3,512,512]{2,1,0:T(8,128)(2,1)} fusion(bf16[3,512,512]{2,1,0:T(8,128)(2,1)S(1)} %copy-done.2, bf16[3,512,512]{2,1,0:T(8,128)(2,1)S(1)} %get-tuple-element.15, pred[3]{0:T(512)(128)(4,1)S(1)} %iota_compare_fusion.3), kind=kOutput, calls=%fused_computation.4 | convolution fusion | flops 810024960 | bytes 4718595 | tf_op jit(solution)/shard_map/sik,sjk->sij/dot_general | solution.py:347
  117.8 8.5 %all-to-all-done.3 = bf16[128,4,8,128]{3,2,1,0:T(8,128)(2,1)S(1)} async-done(((bf16[128,4,8,128]{3,2,1,0:T(8,128)(2,1)}), bf16[128,4,8,128]{3,2,1,0:T(8,128)(2,1)S(1)}, u32[]{:S(2)}, u32[]{:S(2)}) %all-to-all-start.3) | async-done | bytes 1048608 | tf_op jit(solution)/shard_map/all_to_all | solution.py:26
  126.3 1.1 shard_map.124
  (6 shorter events, 0.0 us)
Async XLA Ops:
  2.7 11.5 %copy-start.1 = (s32[256,3]{0,1:T(4,128)S(1)}, s32[256,3]{0,1:T(4,128)}, u32[]{:S(2)}) copy-start(s32[256,3]{0,1:T(4,128)} %param.9) | copy-start | bytes 9220
  2.7 30.7 %all-to-all-start = ((bf16[128,4,8,128]{3,2,1,0:T(8,128)(2,1)}), bf16[128,4,8,128]{3,2,1,0:T(8,128)(2,1)S(1)}, u32[]{:S(2)}, u32[]{:S(2)}) async-start(bf16[128,4,8,128]{3,2,1,0:T(8,128)(2,1)} %bitcast.23), calls=%async_computation | async-start | bytes 2097152 | tf_op jit(solution)/shard_map/all_to_all | solution.py:26
  35.2 29.4 %all-to-all-start.1 = ((bf16[128,3,2,8,128]{4,3,2,1,0:T(8,128)(2,1)}), bf16[128,3,2,8,128]{4,3,2,1,0:T(8,128)(2,1)S(1)}, u32[]{:S(2)}, u32[]{:S(2)}) async-start(bf16[128,3,2,8,128]{4,3,2,1,0:T(8,128)(2,1)} %bitcast.21), calls=%async_computation.1 | async-start | bytes 3145728 | tf_op jit(solution)/shard_map/all_to_all | solution.py:26
  71.5 29.4 %all-to-all-start.2 = ((bf16[128,3,2,8,128]{4,3,2,1,0:T(8,128)(2,1)}), bf16[128,3,2,8,128]{4,3,2,1,0:T(8,128)(2,1)S(1)}, u32[]{:S(2)}, u32[]{:S(2)}) async-start(bf16[128,3,2,8,128]{4,3,2,1,0:T(8,128)(2,1)} %bitcast.24), calls=%async_computation.2 | async-start | bytes 3145728 | tf_op jit(solution)/shard_map/all_to_all | solution.py:26
  102.6 23.8 %all-to-all-start.3 = ((bf16[128,4,8,128]{3,2,1,0:T(8,128)(2,1)}), bf16[128,4,8,128]{3,2,1,0:T(8,128)(2,1)S(1)}, u32[]{:S(2)}, u32[]{:S(2)}) async-start(bf16[128,4,8,128]{3,2,1,0:T(8,128)(2,1)} %bitcast.22), calls=%async_computation.3 | async-start | bytes 2097152 | tf_op jit(solution)/shard_map/all_to_all | solution.py:26
  107.0 4.0 %copy-start = (f32[3,512,512]{2,1,0:T(8,128)S(1)}, f32[3,512,512]{2,1,0:T(8,128)}, u32[]{:S(2)}) copy-start(f32[3,512,512]{2,1,0:T(8,128)} %second_ref.1) | copy-start | bytes 9437188
  111.0 4.5 %copy-start.2 = (bf16[3,512,512]{2,1,0:T(8,128)(2,1)S(1)}, bf16[3,512,512]{2,1,0:T(8,128)(2,1)}, u32[]{:S(2)}) copy-start(bf16[3,512,512]{2,1,0:T(8,128)(2,1)} %param.10) | copy-start | bytes 4718596
